TPU v7x, 32 devices: a whole 2x2x4 slice. The times are simulated.
32 devices in a mesh: seq: 16 (over z, y, core), dp: 2 (over x).
Axes of the slice: x: 2, y: 2, z: 4, core: 2. Of those that a mesh axis runs over, the one named last changes fastest.
Arguments:
- tokens: bfloat16 [2, 2048, 1024], P('dp', 'seq'), may hold values from -6 to 6
- cotangent: bfloat16 [2, 2048, 1024], P('dp', 'seq'), may hold values from -6 to 6
- lengths: int32 [2], replicated, may hold values from 512 to 2048, as said below
- assign: int32 [2], replicated, may hold values from 0 to 1, each once
- w_qkv: bfloat16 [1024, 3072], P(('seq', 'dp')), may hold values from -0.1875 to 0.1875
- qv_bias: bfloat16 [2, 1024], P(None, ('seq', 'dp')), may hold values from -4 to 4
- w_out: bfloat16 [1024, 1024], P(('seq', 'dp')), may hold values from -1.5 to 1.5
- out_bias: bfloat16 [1024], P(('seq', 'dp')), may hold values from -1.5 to 1.5
- w_up: bfloat16 [1024, 4096], P(('seq', 'dp')), may hold values from -0.1875 to 0.1875
- up_bias: bfloat16 [4096], P(('seq', 'dp')), may hold values from -4 to 4
- w_down: bfloat16 [4096, 1024], P(('seq', 'dp')), may hold values from -0.09375 to 0.09375
- down_bias: bfloat16 [1024], P(('seq', 'dp')), may hold values from -3 to 3
- norm_gain: bfloat16 [4, 1024], P(None, ('seq', 'dp')), may hold values from 0.5 to 1.5
- norm_shift: bfloat16 [4, 1024], P(None, ('seq', 'dp')), may hold values from -4 to 4
Outputs:
- output: bfloat16 [2, 2048, 1024], P('dp', 'seq')
- input_grad: bfloat16 [2, 2048, 1024], P('dp', 'seq')
- grad_w_qkv: float32 [1024, 3072], P(('seq', 'dp'))
- grad_qv_bias: float32 [2, 1024], P(None, ('seq', 'dp'))
- grad_w_out: float32 [1024, 1024], P(('seq', 'dp'))
- grad_out_bias: float32 [1024], P(('seq', 'dp'))
- grad_w_up: float32 [1024, 4096], P(('seq', 'dp'))
- grad_up_bias: float32 [4096], P(('seq', 'dp'))
- grad_w_down: float32 [4096, 1024], P(('seq', 'dp'))
- grad_down_bias: float32 [1024], P(('seq', 'dp'))
- grad_norm_gain: float32 [4, 1024], P(None, ('seq', 'dp'))
- grad_norm_shift: float32 [4, 1024], P(None, ('seq', 'dp'))
Inputs may be any that keep to these rules, and one draw needn't show every extreme that they name: `lengths`: each sequence's valid positions; some sequence fills its whole slot of 2048. `assign`: every sequence stands in exactly one slot.
All inputs are finite; a program needn't handle non-finite values.
Results may differ from a plain program's by a relative error of at most 0.01.
Values may be sent and summed in bfloat16 or wider, within the bound.
A program may use at most 192 MiB of HBM per device.

v0:
```python
import math

import jax
import jax.numpy as jnp
from jax import lax
from jax.sharding import PartitionSpec as P

HD = 64


RELAX_SCALE = 32.0
NORM_EPSILON = 1e-05


def norm_rows(values, gain, shift):
    center = values - jnp.mean(values, -1, keepdims=True)
    spread = jnp.mean(center * center, -1, keepdims=True)
    return center * lax.rsqrt(spread + NORM_EPSILON) * gain + shift


def exact_gelu(values):
    return jax.nn.gelu(values, approximate=False)


def contract_rows(left, right):
    return lax.dot_general(
        left, right, (((0,), (0,)), ((), ())), preferred_element_type=jnp.float32
    )


def contract_cols(left, right):
    return lax.dot_general(
        left, right, (((1,), (1,)), ((), ())), preferred_element_type=jnp.float32
    )


def split_heads(block):
    return block.reshape(block.shape[0], 2, HD)


def pair_scores(query_part, key_part):
    factor = 1.0 / (RELAX_SCALE * math.sqrt(HD))
    return (
        jnp.einsum(
            "qhd,khd->hqk",
            split_heads(query_part),
            split_heads(key_part),
            preferred_element_type=jnp.float32,
        )
        * factor
    )


def kept_probs(scores, allowed, row_max, row_total):
    exp_terms = jnp.exp(jnp.where(allowed, RELAX_SCALE * (scores - row_max), -jnp.inf))
    return exp_terms / row_total


def body(
    tokens,
    cotangent,
    lengths,
    assign,
    w_qkv,
    qv_bias,
    w_out,
    out_bias,
    w_up,
    up_bias,
    w_down,
    down_bias,
    norm_gain,
    norm_shift,
):
    gathered = (
        lax.all_gather(w_qkv, ("seq", "dp"), axis=0, tiled=True),
        lax.all_gather(w_out, ("seq", "dp"), axis=0, tiled=True),
        lax.all_gather(w_up, ("seq", "dp"), axis=0, tiled=True),
        lax.all_gather(w_down, ("seq", "dp"), axis=0, tiled=True),
        lax.all_gather(qv_bias, ("seq", "dp"), axis=1, tiled=True),
        lax.all_gather(out_bias, ("seq", "dp"), axis=0, tiled=True),
        lax.all_gather(up_bias, ("seq", "dp"), axis=0, tiled=True),
        lax.all_gather(down_bias, ("seq", "dp"), axis=0, tiled=True),
        lax.all_gather(norm_gain, ("seq", "dp"), axis=1, tiled=True),
        lax.all_gather(norm_shift, ("seq", "dp"), axis=1, tiled=True),
    )
    qkv_full, out_full, up_full, down_full = (gathered[0], gathered[1], gathered[2], gathered[3])
    qv_shift = gathered[4].astype(jnp.float32)
    out_shift = gathered[5].astype(jnp.float32)
    up_shift = gathered[6].astype(jnp.float32)
    down_shift = gathered[7].astype(jnp.float32)
    gains = gathered[8].astype(jnp.float32)
    shifts = gathered[9].astype(jnp.float32)
    row_count = tokens.shape[1]
    model_width = tokens.shape[2]
    pair_cols = 2 * HD
    pair_count = model_width // pair_cols
    slot_rows = row_count * lax.axis_size("seq")
    factor = 1.0 / (RELAX_SCALE * math.sqrt(HD))
    valid = lengths[assign[lax.axis_index("dp")]]
    own_place = lax.axis_index("seq") * row_count + jnp.arange(row_count, dtype=jnp.int32)
    all_place = jnp.arange(slot_rows, dtype=jnp.int32)
    allowed = (all_place[None, :] <= own_place[:, None]) & (all_place[None, :] < valid)
    pair_ids = jnp.arange(pair_count, dtype=jnp.int32)
    hidden = tokens[0].astype(jnp.float32)
    normed_first, pull_first = jax.vjp(norm_rows, hidden, gains[0], shifts[0])
    normed_low = normed_first.astype(jnp.bfloat16)
    projected = jnp.dot(normed_low, qkv_full, preferred_element_type=jnp.float32)
    queries = (projected[:, :model_width] + qv_shift[0]).astype(jnp.bfloat16)
    key_own = projected[:, model_width : 2 * model_width].astype(jnp.bfloat16)
    value_own = (projected[:, 2 * model_width :] + qv_shift[1]).astype(jnp.bfloat16)
    keys, values = (
        lax.all_gather(key_own, "seq", axis=0, tiled=True),
        lax.all_gather(value_own, "seq", axis=0, tiled=True),
    )

    def columns(block, pair_index):
        return lax.dynamic_slice_in_dim(block, pair_index * pair_cols, pair_cols, 1)

    def merge_pairs(stack):
        return stack.transpose(1, 0, 2).reshape(stack.shape[1], model_width)

    def attend(pair_index):
        scores = pair_scores(columns(queries, pair_index), columns(keys, pair_index))
        row_max = jnp.max(jnp.where(allowed, scores, -jnp.inf), -1, keepdims=True)
        exp_terms = jnp.exp(jnp.where(allowed, RELAX_SCALE * (scores - row_max), -jnp.inf))
        row_total = jnp.sum(exp_terms, -1, keepdims=True)
        probs = (exp_terms / row_total).astype(jnp.bfloat16)
        mixed = jnp.einsum(
            "hqk,khd->qhd",
            probs,
            split_heads(columns(values, pair_index)),
            preferred_element_type=jnp.float32,
        )
        return (mixed.reshape(row_count, pair_cols), row_max[..., 0], row_total[..., 0])

    mixed_pairs, max_pairs, total_pairs = lax.map(attend, pair_ids)
    attended = merge_pairs(mixed_pairs).astype(jnp.bfloat16)
    branch = jnp.dot(attended, out_full, preferred_element_type=jnp.float32) + out_shift
    normed_second, pull_second = jax.vjp(norm_rows, branch, gains[1], shifts[1])
    middle = hidden + normed_second
    normed_third, pull_third = jax.vjp(norm_rows, middle, gains[2], shifts[2])
    third_low = normed_third.astype(jnp.bfloat16)
    up_pre = jnp.dot(third_low, up_full, preferred_element_type=jnp.float32) + up_shift
    activated, pull_gelu = jax.vjp(exact_gelu, up_pre)
    active_low = activated.astype(jnp.bfloat16)
    down_pre = jnp.dot(active_low, down_full, preferred_element_type=jnp.float32) + down_shift
    normed_fourth, pull_fourth = jax.vjp(norm_rows, down_pre, gains[3], shifts[3])
    output = (middle + normed_fourth).astype(jnp.bfloat16)[None]
    again = (
        lax.all_gather(w_qkv, ("seq", "dp"), axis=0, tiled=True),
        lax.all_gather(w_out, ("seq", "dp"), axis=0, tiled=True),
        lax.all_gather(w_up, ("seq", "dp"), axis=0, tiled=True),
        lax.all_gather(w_down, ("seq", "dp"), axis=0, tiled=True),
    )
    qkv_back, out_back, up_back, down_back = (again[0], again[1], again[2], again[3])
    keep_rows = (own_place < valid).astype(jnp.float32)[:, None]
    grad_out = cotangent[0].astype(jnp.float32) * keep_rows
    grad_down, grad_gain_four, grad_shift_four = pull_fourth(grad_out)
    grad_down_low = grad_down.astype(jnp.bfloat16)
    grad_w_down = contract_rows(active_low, grad_down_low)
    grad_b_down = jnp.sum(grad_down_low.astype(jnp.float32), 0)
    (grad_up,) = pull_gelu(contract_cols(grad_down_low, down_back))
    grad_up_low = grad_up.astype(jnp.bfloat16)
    grad_w_up = contract_rows(third_low, grad_up_low)
    grad_b_up = jnp.sum(grad_up_low.astype(jnp.float32), 0)
    grad_middle_part, grad_gain_three, grad_shift_three = pull_third(
        contract_cols(grad_up_low, up_back)
    )
    grad_middle = grad_out + grad_middle_part
    grad_branch, grad_gain_two, grad_shift_two = pull_second(grad_middle)
    grad_branch_low = grad_branch.astype(jnp.bfloat16)
    grad_w_out = contract_rows(attended, grad_branch_low)
    grad_b_out = jnp.sum(grad_branch_low.astype(jnp.float32), 0)
    grad_attended = contract_cols(grad_branch_low, out_back).astype(jnp.bfloat16)

    def query_side(pair_index):
        scores = pair_scores(columns(queries, pair_index), columns(keys, pair_index))
        probs = kept_probs(
            scores, allowed, max_pairs[pair_index][..., None], total_pairs[pair_index][..., None]
        )
        grad_part = columns(grad_attended, pair_index)
        grad_probs = jnp.einsum(
            "qhd,khd->hqk",
            split_heads(grad_part),
            split_heads(columns(values, pair_index)),
            preferred_element_type=jnp.float32,
        )
        delta = jnp.sum(probs * grad_probs, -1, keepdims=True)
        grad_scores = (RELAX_SCALE * probs * (grad_probs - delta)).astype(jnp.bfloat16)
        grad_query = (
            jnp.einsum(
                "hqk,khd->qhd",
                grad_scores,
                split_heads(columns(keys, pair_index)),
                preferred_element_type=jnp.float32,
            )
            * factor
        )
        return (grad_query.reshape(row_count, pair_cols), grad_scores, probs, delta)

    def both_sides(pair_index):
        grad_query, grad_scores, probs, delta = query_side(pair_index)
        grad_part = columns(grad_attended, pair_index)
        grad_key = (
            jnp.einsum(
                "hqk,qhd->khd",
                grad_scores,
                split_heads(columns(queries, pair_index)),
                preferred_element_type=jnp.float32,
            )
            * factor
        )
        grad_value = jnp.einsum(
            "hqk,qhd->khd",
            probs.astype(jnp.bfloat16),
            split_heads(grad_part),
            preferred_element_type=jnp.float32,
        )
        return (
            grad_query,
            grad_key.reshape(slot_rows, pair_cols),
            grad_value.reshape(slot_rows, pair_cols),
        )

    query_pairs, key_terms, value_terms = lax.map(both_sides, pair_ids)
    key_pairs, value_pairs = (
        lax.psum_scatter(
            key_terms.astype(jnp.bfloat16), "seq", scatter_dimension=1, tiled=True
        ).astype(jnp.float32),
        lax.psum_scatter(
            value_terms.astype(jnp.bfloat16), "seq", scatter_dimension=1, tiled=True
        ).astype(jnp.float32),
    )
    grad_q_low = merge_pairs(query_pairs).astype(jnp.bfloat16)
    grad_k_low = merge_pairs(key_pairs).astype(jnp.bfloat16)
    grad_v_low = merge_pairs(value_pairs).astype(jnp.bfloat16)
    grad_projected = jnp.concatenate([grad_q_low, grad_k_low, grad_v_low], 1)
    grad_w_qkv = contract_rows(normed_low, grad_projected)
    grad_qv = jnp.stack(
        [jnp.sum(grad_q_low.astype(jnp.float32), 0), jnp.sum(grad_v_low.astype(jnp.float32), 0)]
    )
    grad_hidden_part, grad_gain_one, grad_shift_one = pull_first(
        contract_cols(grad_projected, qkv_back)
    )
    input_grad = (grad_middle + grad_hidden_part).astype(jnp.bfloat16)[None]
    grad_gains = jnp.stack([grad_gain_one, grad_gain_two, grad_gain_three, grad_gain_four])
    grad_shifts = jnp.stack([grad_shift_one, grad_shift_two, grad_shift_three, grad_shift_four])
    owned = (
        lax.psum_scatter(grad_w_qkv, ("seq", "dp"), scatter_dimension=0, tiled=True),
        lax.psum_scatter(grad_w_out, ("seq", "dp"), scatter_dimension=0, tiled=True),
        lax.psum_scatter(grad_w_up, ("seq", "dp"), scatter_dimension=0, tiled=True),
        lax.psum_scatter(grad_w_down, ("seq", "dp"), scatter_dimension=0, tiled=True),
        lax.psum_scatter(grad_qv, ("seq", "dp"), scatter_dimension=1, tiled=True),
        lax.psum_scatter(grad_b_out, ("seq", "dp"), scatter_dimension=0, tiled=True),
        lax.psum_scatter(grad_b_up, ("seq", "dp"), scatter_dimension=0, tiled=True),
        lax.psum_scatter(grad_b_down, ("seq", "dp"), scatter_dimension=0, tiled=True),
        lax.psum_scatter(grad_gains, ("seq", "dp"), scatter_dimension=1, tiled=True),
        lax.psum_scatter(grad_shifts, ("seq", "dp"), scatter_dimension=1, tiled=True),
    )
    return (
        output,
        input_grad,
        owned[0],
        owned[4],
        owned[1],
        owned[5],
        owned[2],
        owned[6],
        owned[3],
        owned[7],
        owned[8],
        owned[9],
    )


def solution(mesh):
    return jax.shard_map(
        body,
        mesh=mesh,
        in_specs=(
            P("dp", "seq", None),
            P("dp", "seq", None),
            P(),
            P(),
            P(("seq", "dp"), None),
            P(None, ("seq", "dp")),
            P(("seq", "dp"), None),
            P(("seq", "dp")),
            P(("seq", "dp"), None),
            P(("seq", "dp")),
            P(("seq", "dp"), None),
            P(("seq", "dp")),
            P(None, ("seq", "dp")),
            P(None, ("seq", "dp")),
        ),
        out_specs=(
            P("dp", "seq", None),
            P("dp", "seq", None),
            P(("seq", "dp"), None),
            P(None, ("seq", "dp")),
            P(("seq", "dp"), None),
            P(("seq", "dp")),
            P(("seq", "dp"), None),
            P(("seq", "dp")),
            P(("seq", "dp"), None),
            P(("seq", "dp")),
            P(None, ("seq", "dp")),
            P(None, ("seq", "dp")),
        ),
        check_vma=False,
    )
```

profile of v0, /device:TPU:0, one launch (start us, length us, event | category | flops | bytes accessed | tf_op | source)
XLA Modules:
  0.0 2243.5 jit_solution(5692575531233275247)
XLA Ops:
  8.0 70.7 %all-gather.1 = bf16[32,32,4]{1,2,0:T(4,128)(2,1)S(1)} all-gather(bf16[1,32,4]{1,2,0:T(4,128)(2,1)} %bitcast.321), channel_id=1, replica_groups=mesh['seq'=16,'dp'=2] {'seq','dp'}, dimensions={0}, use_global_device_ids=true | all-gather | bytes 8448 | tf_op jit(solution)/shard_map/all_gather | solution.py:85
  78.8 63.8 %all-gather = bf16[32,32,4]{1,2,0:T(4,128)(2,1)S(1)} all-gather(bf16[1,32,4]{1,2,0:T(4,128)(2,1)} %bitcast.322), channel_id=1, replica_groups=mesh['seq'=16,'dp'=2] {'seq','dp'}, dimensions={0}, use_global_device_ids=true | all-gather | bytes 8448 | tf_op jit(solution)/shard_map/all_gather | solution.py:84
  142.7 65.7 %all-gather.2 = bf16[32,32,2]{1,2,0:T(2,128)(2,1)S(1)} all-gather(bf16[1,32,2]{1,2,0:T(2,128)(2,1)} %bitcast.323), channel_id=1, replica_groups=mesh['seq'=16,'dp'=2] {'seq','dp'}, dimensions={0}, use_global_device_ids=true | all-gather | bytes 4224 | tf_op jit(solution)/shard_map/all_gather | solution.py:80
  223.3 38.2 %all-reduce.6 = (bf16[1024]{0:T(1024)(128)(2,1)S(1)}, bf16[1024]{0:T(1024)(128)(2,1)S(1)}) all-reduce(bf16[1024]{0:T(1024)(128)(2,1)S(1)} %dynamic-update-slice, bf16[1024]{0:T(1024)(128)(2,1)S(1)} %dynamic-update-slice.1), channel_id=1, replica_groups=mesh['seq'=16,'dp'=2] {'seq','dp'}, use_global_device_ids=true, to_apply=%add | all-reduce | flops 2048 | bytes 8192
  261.5 66.4 %all-gather.3 = bf16[32,1,128]{2,1,0:T(2,128)(2,1)S(1)} all-gather(bf16[1,1,128]{2,1,0:T(2,128)(2,1)S(1)} %bitcast.324), channel_id=1, replica_groups=mesh['seq'=16,'dp'=2] {'seq','dp'}, dimensions={0}, use_global_device_ids=true | all-gather | bytes 8448 | tf_op jit(solution)/shard_map/all_gather | solution.py:82
  328.1 6.6 copy.56
  334.7 6.5 copy.58
  341.3 46.6 %while.30 = (s32[]{:T(128)}, bf16[8,128,128]{1,2,0:T(8,128)(2,1)S(1)}, f32[8,2,128]{2,1,0:T(2,128)S(1)}, f32[8,2,128]{2,1,0:T(2,128)S(1)}, s32[8]{0:T(128)S(1)},...) while((s32[]{:T(128)}, ...), condition=%wide.region_5.6_spmd.clone, body=%wide.region_2.5_spmd.clone.sunk | while | flops 141032960 | bytes 10694363 | solution.py:137
  391.4 59.3 %all-gather.19.cloned.1.call-done = bf16[1024,4096]{1,0:T(8,128)(2,1)} async-done(((bf16[32,4096]{1,0:T(8,128)(2,1)}), bf16[1024,4096]{1,0:T(8,128)(2,1)}) %all-gather.19.cloned.1.call-update) | async-done | bytes 8388624 | tf_op jit(solution)/shard_map/all_gather | solution.py:78
  450.8 9.6 multiply_convert_fusion.1
  460.4 69.0 %all-gather.21.cloned.1.call-done = bf16[4096,1024]{1,0:T(8,128)(2,1)} async-done(((bf16[128,1024]{1,0:T(8,128)(2,1)}), bf16[4096,1024]{1,0:T(8,128)(2,1)}) %all-gather.21.cloned.1.call-update) | async-done | bytes 8388624 | tf_op jit(solution)/shard_map/all_gather | solution.py:79
  529.4 4.9 fusion.75
  536.1 5.3 convert_reduce_fusion
  548.9 96.1 %while.31 = (s32[]{:T(128)}, bf16[8,128,128]{1,2,0:T(8,128)(2,1)}, bf16[8,2048,128]{1,2,0:T(8,128)(2,1)}, bf16[8,2048,128]{1,2,0:T(8,128)(2,1)}, s32[8]{0:T(128)...) while((s32[]{:T(128)}, bf16[8,128,128]{1,2,0:T(8,128)(2,1)}, ...), condition=%wide.region_20.21_spmd.clone, body=%wide.region_18.20_spmd.clone.sunk | while | flops 342916864 | bytes 23505704 | solution.py:226
  645.1 7.0 copy.65
  652.0 5.3 copy.83
  657.4 6.8 copy.63
  664.2 5.4 copy.84
  670.7 58.2 %reduce-scatter.30.cloned.1.call-done = bf16[128,1024]{1,0:T(8,128)(2,1)} async-done(((bf16[2048,1024]{1,0:T(8,128)(2,1)}), bf16[128,1024]{1,0:T(8,128)(2,1)}) %reduce-scatter.30.cloned.1.call-update) | async-done | bytes 262160
  730.1 74.5 %reduce-scatter.28.cloned.1.call-done = bf16[128,1024]{1,0:T(8,128)(2,1)} async-done(((bf16[2048,1024]{1,0:T(8,128)(2,1)}), bf16[128,1024]{1,0:T(8,128)(2,1)}) %reduce-scatter.28.cloned.1.call-update) | async-done | bytes 262160
  806.0 5.1 fusion.63
  817.6 6.4 fusion.48
  825.2 8.2 fusion.62
  834.7 8.1 fusion.78
  842.8 39.9 %all-reduce.5 = (f32[1024]{0:T(1024)S(1)}, f32[4096]{0:T(1024)S(1)}, f32[1024]{0:T(1024)S(1)}) all-reduce(f32[1024]{0:T(1024)S(1)} %get-tuple-element.345, f32[4096]{0:T(1024)S(1)} %get-tuple-element.343, f32[1024]{0:T(1024)S(1)} %get-tuple-element.341), channel_id=7, replica_groups=mesh['seq'=16,'dp'=2] {'seq','dp'}, use_global_device_ids=true, to_apply=%region_31.32.clone | all-reduce | flops 6144 | bytes 49152
  885.4 62.1 %reduce-scatter.32.cloned.1.call-done = f32[32,2]{1,0:T(8,128)} async-done(((f32[1024,2]{1,0:T(8,128)}), f32[32,2]{1,0:T(8,128)}) %reduce-scatter.32.cloned.1.call-update) | async-done | bytes 272
  948.8 132.3 %reduce-scatter.34.cloned.1.call-done = f32[32,4]{1,0:T(8,128)} async-done(((f32[1024,4]{1,0:T(8,128)}), f32[32,4]{1,0:T(8,128)}) %reduce-scatter.34.cloned.1.call-update) | async-done | bytes 528
  1082.5 132.6 %reduce-scatter.36.cloned.1.call-done = f32[32,4]{1,0:T(8,128)} async-done(((f32[1024,4]{1,0:T(8,128)}), f32[32,4]{1,0:T(8,128)}) %reduce-scatter.36.cloned.1.call-update) | async-done | bytes 528
  1216.5 141.1 %reduce-scatter.22.cloned.1.call-done = f32[32,1024]{1,0:T(8,128)} async-done(((f32[1024,1024]{1,0:T(8,128)}), f32[32,1024]{1,0:T(8,128)}) %reduce-scatter.22.cloned.1.call-update) | async-done | bytes 131088 | tf_op jit(solution)/shard_map/reduce_scatter | solution.py:251
  1357.6 158.6 %reduce-scatter.20.cloned.1.call-done = f32[32,3072]{1,0:T(8,128)} async-done(((f32[1024,3072]{1,0:T(8,128)}), f32[32,3072]{1,0:T(8,128)}) %reduce-scatter.20.cloned.1.call-update) | async-done | bytes 393232 | tf_op jit(solution)/shard_map/reduce_scatter | solution.py:250
  1516.1 359.0 %reduce-scatter.24.cloned.1.call-done = f32[32,4096]{1,0:T(8,128)} async-done(((f32[1024,4096]{1,0:T(8,128)}), f32[32,4096]{1,0:T(8,128)}) %reduce-scatter.24.cloned.1.call-update) | async-done | bytes 524304 | tf_op jit(solution)/shard_map/reduce_scatter | solution.py:252
  1875.1 361.5 %reduce-scatter.26.cloned.1.call-done = f32[128,1024]{1,0:T(8,128)} async-done(((f32[4096,1024]{1,0:T(8,128)}), f32[128,1024]{1,0:T(8,128)}) %reduce-scatter.26.cloned.1.call-update) | async-done | bytes 524304 | tf_op jit(solution)/shard_map/reduce_scatter | solution.py:253
  (392 shorter events, 161.7 us)
Async XLA Ops:
  7.2 203.7 %all-gather.11.cloned.1.call-start = ((), (), s32[]{:S(2)}) async-start(), calls=%async_computation.9 | async-start | bytes 6488064 | tf_op jit(solution)/shard_map/all_gather | solution.py:76
  7.9 320.2 %all-gather.13.cloned.1.call-start = ((), (), s32[]{:S(2)}) async-start(), calls=%async_computation.10 | async-start | bytes 4456448 | tf_op jit(solution)/shard_map/all_gather | solution.py:114
  214.8 3.5 copy-start.18
  214.8 6.1 copy-start.19
  214.8 8.0 copy-start.20
  214.9 8.3 copy-start.21
  214.9 46.6 %copy-start.17 = (bf16[128]{0:T(256)(128)(2,1)S(1)}, bf16[128]{0:T(256)(128)(2,1)}, u32[]{:S(2)}) copy-start(bf16[128]{0:T(256)(128)(2,1)} %param.27) | copy-start | bytes 772
  215.7 119.0 %all-gather.15.cloned.1.call-start = ((), (), s32[]{:S(2)}) async-start(), calls=%async_computation.11 | async-start | bytes 4456448 | tf_op jit(solution)/shard_map/all_gather | solution.py:113
  216.5 171.4 %all-gather.17.cloned.1.call-start = ((), (), s32[]{:S(2)}) async-start(), calls=%async_computation.12 | async-start | bytes 2162688 | tf_op jit(solution)/shard_map/all_gather | solution.py:77
  217.1 233.7 %all-gather.19.cloned.1.call-start = ((), (), s32[]{:S(2)}) async-start(), calls=%async_computation.13 | async-start | bytes 8650752 | tf_op jit(solution)/shard_map/all_gather | solution.py:78
  217.7 311.6 %all-gather.21.cloned.1.call-start = ((), (), s32[]{:S(2)}) async-start(), calls=%async_computation.14 | async-start | bytes 8650752 | tf_op jit(solution)/shard_map/all_gather | solution.py:79
  218.3 510.6 %reduce-scatter.30.cloned.1.call-start = ((), (), s32[]{:S(2)}) async-start(), calls=%async_computation.20 | async-start | bytes 4456448
  387.9 3.3 copy-start.8
  460.4 73.8 %copy-start.2 = (bf16[128,4096]{1,0:T(8,128)(2,1)}, bf16[128,4096]{1,0:T(8,128)(2,1)S(1)}, u32[]{:S(2)}) copy-start(bf16[128,4096]{1,0:T(8,128)(2,1)S(1)} %get-tuple-element.354) | copy-start | bytes 3145732
  529.3 6.6 slice-start
  529.4 5.1 copy-start.13
  529.4 6.6 slice-start.1
  534.8 6.6 slice-start.2
  536.0 5.4 copy-start.15
  536.1 5.3 slice-start.3
  541.4 3.2 copy-start.6
  657.4 147.2 %reduce-scatter.28.cloned.1.call-start = ((), (), s32[]{:S(2)}) async-start(), calls=%async_computation.19 | async-start | bytes 4456448
  669.7 277.8 %reduce-scatter.32.cloned.1.call-start = ((), (), s32[]{:S(2)}) async-start(), calls=%async_computation.21 | async-start | bytes 540672
  811.0 3.8 copy-start.9
  811.1 3.8 copy-start.11
  812.2 269.0 %reduce-scatter.34.cloned.1.call-start = ((), (), s32[]{:S(2)}) async-start(), calls=%async_computation.22 | async-start | bytes 540672
  813.6 401.4 %reduce-scatter.36.cloned.1.call-start = ((), (), s32[]{:S(2)}) async-start(), calls=%async_computation.23 | async-start | bytes 540672
  814.8 542.8 %reduce-scatter.22.cloned.1.call-start = ((), (), s32[]{:S(2)}) async-start(), calls=%async_computation.16 | async-start | bytes 4325376 | tf_op jit(solution)/shard_map/reduce_scatter | solution.py:251
  817.5 698.6 %reduce-scatter.20.cloned.1.call-start = ((), (), s32[]{:S(2)}) async-start(), calls=%async_computation.15 | async-start | bytes 12976128 | tf_op jit(solution)/shard_map/reduce_scatter | solution.py:250
  824.0 1051.1 %reduce-scatter.24.cloned.1.call-start = ((), (), s32[]{:S(2)}) async-start(), calls=%async_computation.17 | async-start | bytes 17301504 | tf_op jit(solution)/shard_map/reduce_scatter | solution.py:252
  833.4 1403.1 %reduce-scatter.26.cloned.1.call-start = ((), (), s32[]{:S(2)}) async-start(), calls=%async_computation.18 | async-start | bytes 17301504 | tf_op jit(solution)/shard_map/reduce_scatter | solution.py:253
  842.8 41.6 %copy-start.5 = (f32[128,1024]{1,0:T(8,128)S(1)}, f32[128,1024]{1,0:T(8,128)}, u32[]{:S(2)}) copy-start(f32[128,1024]{1,0:T(8,128)} %copy-done.4) | copy-start | bytes 1572868
  (10 other events, 14.9 us)
Sparse Core Ops, SparseCore 0:
  10.9 72.2 all-gather.10
  215.8 46.5 all-gather.12
  265.2 48.9 all-gather.14
  317.0 54.8 all-gather.16
  374.8 75.9 all-gather.18
  453.6 75.6 all-gather.20
  657.5 71.3 reduce-scatter.29
  732.7 71.8 reduce-scatter.27
  812.3 135.1 reduce-scatter.31
  949.6 131.4 reduce-scatter.33
  1083.4 131.6 reduce-scatter.35
  1217.8 139.7 reduce-scatter.21
  1364.2 151.9 reduce-scatter.19
  1518.8 356.2 reduce-scatter.23
  1877.8 358.6 reduce-scatter.25
where the time goes:
time: 2260 us; the launch traced here: 2240 us
  waiting for transfers between devices  1610 us (71%)
  blocking collectives  345 us (15%)
  local copies, waits for them, and re-layouts  129 us (6%)
  matrix products  93.9 us (4%)
  loops' own time  27.1 us (1%)
    unnamed x20, waiting for transfers between devices  462 us
    reduce_scatter x1, waiting for transfers between devices, body(): lax.psum_scatter(grad_w_down, ('seq', 'dp'), scatter_dimension=0, tiled=T...  361 us
    reduce_scatter x1, waiting for transfers between devices, body(): lax.psum_scatter(grad_w_up, ('seq', 'dp'), scatter_dimension=0, tiled=True)  359 us
    reduce_scatter x1, waiting for transfers between devices, body(): lax.psum_scatter(grad_w_qkv, ('seq', 'dp'), scatter_dimension=0, tiled=True)  159 us
    reduce_scatter x1, waiting for transfers between devices, body(): lax.psum_scatter(grad_w_out, ('seq', 'dp'), scatter_dimension=0, tiled=True)  141 us
    unnamed x2, blocking collectives  78 us
    all_gather x1, blocking collectives, body(): lax.all_gather(norm_shift, ('seq', 'dp'), axis=1, tiled=True)  70.7 us
    all_gather x1, waiting for transfers between devices, body(): lax.all_gather(w_down, ('seq', 'dp'), axis=0, tiled=True)  69 us
  transfers between devices with their start and end apart: 15, of which 11 were waited for; matrix products, arithmetic and copies ran while one was open for 5% of the time, Pallas kernels for 0%

commit v1 on v0

--- a/solution.py
+++ b/solution.py
@@ -1,9 +1,13 @@
+import functools
 import math
 
 import jax
 import jax.numpy as jnp
 from jax import lax
+from jax.experimental import pallas as pl
+from jax.experimental.pallas import tpu as pltpu
 from jax.sharding import PartitionSpec as P
+
 
 HD = 64
 
@@ -274,9 +278,451 @@
     )
 
 
+MESH = pl.DeviceIdType.MESH
+
+
+def is_small(mesh):
+    return mesh.shape["seq"] == 16 and mesh.shape["dp"] == 2
+
+
+def place():
+    seq = lax.axis_index("seq")
+    return seq // 8, (seq // 4) % 2, (seq // 2) % 2, seq % 2, lax.axis_index("dp")
+
+
+def exchange_kernel(scatter, src, out, send_sem, recv_sem, own_sem):
+    a, b, y, c, x = place()
+    barrier = pltpu.get_barrier_semaphore()
+
+    def peer(k):
+        return lax.rem(a + k // 2, 2), lax.rem(y + k % 2, 2)
+
+    def device(k):
+        pa, py = peer(k)
+        return (pa * 8 + b * 4 + py * 2 + c, x)
+
+    def source(k):
+        pa, py = peer(k)
+        return src.at[pa * 2 + py] if scatter else src.at[pa, :, py]
+
+    def target(k):
+        pa, py = peer(k)
+        return out.at[pa, :, py] if scatter else out.at[pa * 2 + py]
+
+    for k in range(1, 4):
+        pl.semaphore_signal(barrier, inc=1, device_id=device(k), device_id_type=MESH)
+    own = pltpu.make_async_copy(source(0), target(0), own_sem)
+    own.start()
+    pl.semaphore_wait(barrier, 3)
+
+    def copy(k, dst):
+        return pltpu.make_async_remote_copy(
+            src_ref=source(k), dst_ref=target(dst), send_sem=send_sem.at[k], recv_sem=recv_sem.at[k],
+            device_id=device(k), device_id_type=MESH)
+
+    for k in (3, 2, 1):
+        copy(k, 0).start()
+    own.wait()
+    for k in (3, 2, 1):
+        copy(k, k).wait_recv()
+    for k in (3, 2, 1):
+        copy(k, 0).wait_send()
+
+
+def exchange(blocks, scatter, cid):
+    vm = pl.BlockSpec(memory_space=pltpu.VMEM)
+    rows = blocks.shape[-2]
+    shape = (2, 2, 2, rows, 128) if scatter else (4, 2, rows, 128)
+    return pl.pallas_call(
+        functools.partial(exchange_kernel, scatter), out_shape=jax.ShapeDtypeStruct(shape, blocks.dtype),
+        in_specs=[vm], out_specs=vm,
+        scratch_shapes=[pltpu.SemaphoreType.DMA((4,)), pltpu.SemaphoreType.DMA((4,)), pltpu.SemaphoreType.DMA],
+        compiler_params=pltpu.CompilerParams(collective_id=cid, has_side_effects=True),
+        cost_estimate=pl.CostEstimate(flops=0, bytes_accessed=rows * 100000, transcendentals=0),
+        name="exchange",
+    )(blocks)
+
+
+def dot_nt(a, b):
+    return lax.dot_general(a, b, (((1,), (1,)), ((), ())), preferred_element_type=jnp.float32)
+
+
+def dot_nn(a, b):
+    return jnp.dot(a, b, preferred_element_type=jnp.float32)
+
+
+BQ = 256
+MASKED = -1e30
+
+
+def load_heads(valid, packed, q_ref, k_ref):
+    rows = q_ref.shape[0]
+    qk = packed[:, :256].reshape(rows, 128)
+    kq = jnp.concatenate([qk[:, 64:], qk[:, :64]], axis=1)
+    lane = lax.broadcasted_iota(jnp.int32, (rows, 128), 1)
+    spot = lax.broadcasted_iota(jnp.int32, (rows, 128), 0)
+    past = jnp.where(spot < valid, 0.0, MASKED)
+    q_ref[...] = jnp.where(lane < 64, qk.astype(jnp.float32), jnp.where(lane == 64, 1.0, 0.0)).astype(jnp.bfloat16)
+    k_ref[...] = jnp.where(lane < 64, kq.astype(jnp.float32), jnp.where(lane == 64, past, 0.0)).astype(jnp.bfloat16)
+
+
+def unpack_rows(halves):
+    n = halves.shape[0]
+    return jnp.concatenate([halves[:, :, :64], halves[:, :, 64:]], axis=1).reshape(n * 256, 64)
+
+
+def block_probs(q_ref, k_ref, i):
+    n = (i + 1) * BQ
+    scores = dot_nt(k_ref[:n], q_ref[i * BQ:n])
+    key = lax.broadcasted_iota(jnp.int32, (BQ, BQ), 0)
+    query = lax.broadcasted_iota(jnp.int32, (BQ, BQ), 1)
+    corner = jnp.where(key <= query, scores[n - BQ:], MASKED)
+    scores = jnp.concatenate([scores[:n - BQ], corner], axis=0) if i else corner
+    top = jnp.max(scores, axis=0, keepdims=True)
+    terms = jnp.exp((scores - top) * 0.125)
+    return terms, 1.0 / jnp.sum(terms, axis=0, keepdims=True)
+
+
+def attend_kernel(valid_ref, packed, out_ref, q_ref, k_ref, vt_ref):
+    load_heads(valid_ref[0], packed, q_ref, k_ref)
+    unit = jnp.where(
+        lax.broadcasted_iota(jnp.int32, (64, 64), 0) == lax.broadcasted_iota(jnp.int32, (64, 64), 1), 1.0, 0.0
+    ).astype(jnp.bfloat16)
+    vt_ref[...] = dot_nt(unit, unpack_rows(packed[:, 256:])).astype(jnp.bfloat16)
+    for i in range(q_ref.shape[0] // BQ):
+        n = (i + 1) * BQ
+        terms, scale = block_probs(q_ref, k_ref, i)
+        probs = (terms * scale).astype(jnp.bfloat16)
+        mixed = dot_nn(vt_ref[:, :n], probs).T
+        out_ref[i] = jnp.concatenate([mixed[:128], mixed[128:]], axis=1).astype(jnp.bfloat16)
+
+
+def attend_back_kernel(valid_ref, packed, grad, out_ref, q_ref, k_ref, v_ref, g_ref, kt_ref, dk_ref, dv_ref):
+    load_heads(valid_ref[0], packed, q_ref, k_ref)
+    v_ref[...] = unpack_rows(packed[:, 256:])
+    g_ref[...] = unpack_rows(grad[...])
+    unit = jnp.where(
+        lax.broadcasted_iota(jnp.int32, (64, 128), 0) == lax.broadcasted_iota(jnp.int32, (64, 128), 1), 1.0, 0.0
+    ).astype(jnp.bfloat16)
+    kt_ref[...] = dot_nt(unit, k_ref[...]).astype(jnp.bfloat16)
+    dk_ref[...] = jnp.zeros_like(dk_ref)
+    dv_ref[...] = jnp.zeros_like(dv_ref)
+    blocks = q_ref.shape[0] // BQ
+    for i in range(blocks):
+        n = (i + 1) * BQ
+        terms, scale = block_probs(q_ref, k_ref, i)
+        probs = terms * scale
+        grad_probs = dot_nt(v_ref[:n], g_ref[i * BQ:n])
+        delta = jnp.sum(probs * grad_probs, axis=0, keepdims=True)
+        grad_scores = (probs * (grad_probs - delta)).astype(jnp.bfloat16)
+        grad_query = dot_nn(kt_ref[:, :n], grad_scores).T * 0.125
+        out_ref[i, :256, :64] = grad_query.astype(jnp.bfloat16)
+        dk_ref[:n] += dot_nn(grad_scores, q_ref[i * BQ:n])
+        dv_ref[:n] += dot_nn(probs.astype(jnp.bfloat16), g_ref[i * BQ:n])
+    for i in range(blocks):
+        rows = slice(i * BQ, (i + 1) * BQ)
+        out_ref[i, :256, 64:] = (dk_ref[rows, :64] * 0.125).astype(jnp.bfloat16)
+        value = dv_ref[rows].astype(jnp.bfloat16)
+        out_ref[i, 256:] = jnp.concatenate([value[:128], value[128:]], axis=1)
+
+
+def attend(valid, packed):
+    rows = packed.shape[0] * 256
+    vm = pl.BlockSpec(memory_space=pltpu.VMEM)
+    return pl.pallas_call(
+        attend_kernel,
+        out_shape=jax.ShapeDtypeStruct((packed.shape[0], 128, 128), jnp.bfloat16),
+        in_specs=[pl.BlockSpec(memory_space=pltpu.SMEM), vm], out_specs=vm,
+        scratch_shapes=[pltpu.VMEM((rows, 128), jnp.bfloat16)] * 2 + [pltpu.VMEM((64, rows), jnp.bfloat16)],
+        compiler_params=pltpu.CompilerParams(vmem_limit_bytes=48 << 20),
+        name="attend",
+    )(valid, packed)
+
+
+def attend_back(valid, packed, grad):
+    rows = packed.shape[0] * 256
+    vm = pl.BlockSpec(memory_space=pltpu.VMEM)
+    return pl.pallas_call(
+        attend_back_kernel,
+        out_shape=jax.ShapeDtypeStruct(packed.shape, jnp.bfloat16),
+        in_specs=[pl.BlockSpec(memory_space=pltpu.SMEM), vm, vm], out_specs=vm,
+        scratch_shapes=[pltpu.VMEM((rows, 128), jnp.bfloat16)] * 2 + [pltpu.VMEM((rows, 64), jnp.bfloat16)] * 2
+        + [pltpu.VMEM((64, rows), jnp.bfloat16), pltpu.VMEM((rows, 128), jnp.float32), pltpu.VMEM((rows, 64), jnp.float32)],
+        compiler_params=pltpu.CompilerParams(vmem_limit_bytes=48 << 20),
+        name="attend_back",
+    )(valid, packed, grad)
+
+
+def flip(bits, block):
+    return lax.ppermute(block, "seq", [(s, s ^ bits) for s in range(16)])
+
+
+flip_a, flip_b, flip_y, flip_core, flip_far = (functools.partial(flip, bits) for bits in (8, 4, 2, 1, 5))
+
+
+def flip_x(block):
+    return lax.ppermute(block, "dp", [(0, 1), (1, 0)])
+
+
+def after(value, *others):
+    return lax.optimization_barrier((value,) + others)[0]
+
+
+def pick(block, index, axis, keepdims=False):
+    return lax.dynamic_index_in_dim(block, index, axis, keepdims=keepdims)
+
+
+def swap_if(flag, block, axis):
+    return jnp.where(flag == 0, block, lax.rev(block, (axis,)))
+
+
+def sort_ranks(block, b, c):
+    return swap_if(c, swap_if(b, block, 0), 1)
+
+
+def to_ranks(block, b, c):
+    mine = pick(pick(block, b, 0), c, 0)
+    core = flip_core(pick(pick(block, b, 0), 1 - c, 0))
+    near = flip_b(pick(pick(block, 1 - b, 0), c, 0))
+    far = flip_far(pick(pick(block, 1 - b, 0), 1 - c, 0))
+    return jnp.stack([jnp.stack([mine, core]), jnp.stack([near, far])])
+
+
+def gather_rows(block):
+    core, near = flip_core(block), flip_b(block)
+    return jnp.concatenate([block, core, near, flip_core(near)], 0)
+
+
+def scatter_rows(part):
+    part = part.reshape(2, 2, part.shape[0] // 4, part.shape[1])
+    far = part[1, 0] + flip_core(part[1, 1])
+    near = part[0, 0] + flip_core(part[0, 1])
+    return near + flip_b(far.astype(jnp.bfloat16)).astype(jnp.float32)
+
+
+def cube_start(block):
+    return jnp.stack([block, flip_a(block)])
+
+
+def cube_one(flip_one, block):
+    return jnp.concatenate([block, flip_one(block)], 0)
+
+
+def arrange_kernel(count, spot_ref, *refs):
+    for k in range(count):
+        block, out = refs[k], refs[count + k]
+        if len(out.shape) == 7:
+            for i in range(2):
+                for j in range(2):
+                    out[0, i, 0, j, 0] = block[0, i, j]
+        else:
+            out[0, 0, 0] = block[0]
+
+
+def arrange(spot, blocks):
+    def coords(i, r, y_first):
+        second, first, a = i // 4, (i // 2) % 2, i % 2
+        y, x = (first, second) if y_first else (second, first)
+        return lax.rem(r[0] + a, 2), lax.rem(r[1] + y, 2), lax.rem(r[2] + x, 2)
+
+    def specs(block, y_first):
+        shape = block.shape
+        if len(shape) == 5:
+            def out_place(i, r):
+                a, y, x = coords(i, r, y_first)
+                return a, 0, y, 0, x, 0, 0
+            return (pl.BlockSpec((1,) + shape[1:], lambda i, r: (i, 0, 0, 0, 0)),
+                    pl.BlockSpec((1, 2, 1, 2, 1) + shape[3:], out_place),
+                    jax.ShapeDtypeStruct((2,) * 5 + shape[3:], block.dtype))
+
+        def out_place(i, r):
+            return coords(i, r, y_first) + (0, 0)
+        return (pl.BlockSpec((1,) + shape[1:], lambda i, r: (i, 0, 0)),
+                pl.BlockSpec((1, 1, 1) + shape[1:], out_place),
+                jax.ShapeDtypeStruct((2, 2, 2) + shape[1:], block.dtype))
+
+    made = [specs(*entry) for entry in blocks]
+    return pl.pallas_call(
+        functools.partial(arrange_kernel, len(blocks)),
+        out_shape=tuple(m[2] for m in made),
+        grid_spec=pltpu.PrefetchScalarGridSpec(
+            num_scalar_prefetch=1, grid=(8,), in_specs=[m[0] for m in made], out_specs=tuple(m[1] for m in made)),
+        compiler_params=pltpu.CompilerParams(vmem_limit_bytes=32 << 20),
+        cost_estimate=pl.CostEstimate(flops=0, bytes_accessed=8 << 20, transcendentals=0),
+        name="arrange",
+    )(spot, *[entry[0] for entry in blocks])
+
+
+def add_low(mine, other):
+    return (mine.astype(jnp.float32) + other.astype(jnp.float32)).astype(jnp.bfloat16)
+
+
+def fold(terms, flip_one, index, axis):
+    return add_low(pick(terms, index, axis, True), flip_one(pick(terms, 1 - index, axis, True)))
+
+
+def fold_last(terms, flip_one, index, axis):
+    return (pick(terms, index, axis, True).astype(jnp.float32)
+            + flip_one(pick(terms, 1 - index, axis, True)).astype(jnp.float32))
+
+
+def pack_heads(block, b, c):
+    block = sort_ranks(block.reshape(2, 2, 128, 4, HD), b, c)
+    return block.transpose(3, 0, 2, 1, 4).reshape(4, 2, 128, 128)
+
+
+def unpack_heads(packed):
+    return packed.reshape(4, 2, 128, 2, HD).transpose(1, 3, 2, 0, 4).reshape(2, 2, 128, 4 * HD)
+
+
+def fast_body(tokens, cotangent, lengths, assign, w_qkv, qv_bias, w_out, out_bias, w_up, up_bias, w_down, down_bias,
+              norm_gain, norm_shift):
+    bf16, f32 = jnp.bfloat16, jnp.float32
+    a, b, y, c, x = place()
+    spot = jnp.stack([a, y, x]).astype(jnp.int32)
+    width = tokens.shape[2]
+    valid = lengths[assign[x]].astype(jnp.int32)
+
+    qkv = w_qkv.reshape(32, 3, 2, 2, 2, 2, HD)
+    qk_ranks = qkv[:, :2].transpose(3, 5, 0, 2, 4, 1, 6).reshape(2, 2, 32, 512)
+    v_ranks = qkv[:, 2].transpose(2, 4, 0, 1, 3, 5).reshape(2, 2, 32, 256)
+    qkv_block = to_ranks(jnp.concatenate([qk_ranks, v_ranks], 3), b, c)
+    small = jnp.concatenate([qv_bias.reshape(-1), out_bias, down_bias, norm_gain.reshape(-1), norm_shift.reshape(-1), up_bias])
+    small = jnp.pad(small.reshape(4, 128), ((0, 12), (0, 0)))
+    small_core, small_near = flip_core(small), flip_b(small)
+    small = jnp.stack([small, small_core, small_near, flip_core(small_near)]).reshape(2, 2, 16, 128)
+
+    qkv_block = sort_ranks(qkv_block, b, c)
+    qk_one, v_one = cube_start(qkv_block[..., :512]), cube_start(qkv_block[..., 512:])
+    out_one, small = cube_start(w_out), cube_start(small)
+    rows = gather_rows(tokens[0])
+    qk_two, v_two, out_two, small = cube_one(flip_y, qk_one), cube_one(flip_x, v_one), cube_one(flip_x, out_one), cube_one(flip_y, small)
+    qk_all, v_all, out_all, small = cube_one(flip_x, qk_two), cube_one(flip_y, v_two), cube_one(flip_y, out_two), cube_one(flip_x, small)
+    wqk, wv, wo = arrange(spot, [(qk_all, True), (v_all, False), (out_all, False)])
+    wqk, wv, wo = wqk.reshape(width, 512), wv.reshape(width, 256), wo.reshape(256, width)
+
+    up = w_up.reshape(32, 2, 2, 2, 2, 2, 128).transpose(2, 4, 0, 1, 3, 5, 6).reshape(2, 2, 32, 1024)
+    up_block = sort_ranks(to_ranks(after(up, qkv_block), b, c), b, c)
+    up_one, down_one = cube_start(after(up_block, qk_one)), cube_start(after(w_down, qk_one))
+    up_two, down_two = cube_one(flip_y, after(up_one, qk_all)), cube_one(flip_x, after(down_one, v_all))
+
+    small = small.reshape(2, 2, 2, 2, 2, 16, 128).astype(f32)
+    for axis, flag in enumerate((x, y, a, b, c)):
+        small = swap_if(flag, small, axis)
+    small = small.transpose(2, 3, 1, 4, 0, 5, 6)[..., :4, :]
+    vectors = small[..., :3, :].reshape(32, 12, 32).transpose(1, 0, 2).reshape(12, width)
+    qv_half = pick(pick(vectors[:2].reshape(2, 2, 2, 2, 2, HD), b, 2), c, 3).reshape(2, 4, HD)
+    qk_shift = jnp.concatenate([qv_half[0], jnp.zeros((4, HD), f32)], 1).reshape(512)
+    v_shift = qv_half[1].reshape(256)
+    out_full, down_full, gains, shifts = vectors[2], vectors[3], vectors[4:8], vectors[8:12]
+    up_shift = pick(pick(small[..., 3, :], b, 1), c, 2).reshape(1024)
+
+    hidden = tokens[0].astype(f32)
+    first = norm_rows(rows.astype(f32), gains[0], shifts[0]).astype(bf16)
+    qk = (dot_nn(first, wqk) + qk_shift).astype(bf16)
+    v = (dot_nn(first, wv) + v_shift).astype(bf16)
+    qk = sort_ranks(qk.reshape(2, 2, 128, 4, 128), b, c).transpose(3, 0, 1, 2, 4).reshape(4, 2, 256, 128)
+    packed = exchange(jnp.concatenate([qk, pack_heads(v, b, c)], 2), True, 1).reshape(8, 384, 128)
+    attended = exchange(attend(valid[None], packed).reshape(2, 2, 2, 128, 128), False, 2)
+    attended = sort_ranks(unpack_heads(attended), b, c).reshape(512, 256)
+
+    up_all, down_all = cube_one(flip_x, up_two), cube_one(flip_y, after(down_two, attended))
+    branch = scatter_rows(dot_nn(attended, wo)) + out_full
+    second, pull_second = jax.vjp(norm_rows, branch, gains[1], shifts[1])
+    middle = hidden + second
+    third, pull_third = jax.vjp(norm_rows, middle, gains[2], shifts[2])
+    third = gather_rows(third.astype(bf16))
+    wu, wd = arrange(spot, [(up_all, True), (down_all, False)])
+    wu, wd = wu.reshape(width, 1024), wd.reshape(1024, width)
+    up_pre = dot_nn(third, wu) + up_shift
+    active, pull_gelu = jax.vjp(exact_gelu, up_pre)
+    active = active.astype(bf16)
+    down_pre = scatter_rows(dot_nn(active, wd)) + down_full
+    fourth, pull_fourth = jax.vjp(norm_rows, down_pre, gains[3], shifts[3])
+    output = (middle + fourth).astype(bf16)
+
+    own_spot = lax.axis_index("seq") * 128 + jnp.arange(128, dtype=jnp.int32)
+    grad_out = cotangent[0].astype(f32) * (own_spot < valid).astype(f32)[:, None]
+    grad_down, gain4, shift4 = pull_fourth(grad_out)
+    grad_down = grad_down.astype(bf16)
+    down_rows = gather_rows(grad_down)
+    gw_down = contract_rows(active, down_rows).astype(bf16).reshape(2, 2, 2, 128, width)
+    down_sum = fold(gw_down, flip_y, y, 1)
+    (grad_up,) = pull_gelu(dot_nt(down_rows, wd))
+    grad_up = grad_up.astype(bf16)
+    gw_up = contract_rows(third, grad_up).astype(bf16).reshape(2, 2, 2, 2, 2, 32, 1024)
+    up_sum = fold(gw_up, flip_x, x, 4)
+    part, gain3, shift3 = pull_third(scatter_rows(dot_nt(grad_up, wu)))
+    grad_middle = grad_out + part
+    grad_branch, gain2, shift2 = pull_second(grad_middle)
+    grad_branch = grad_branch.astype(bf16)
+    branch_rows = gather_rows(grad_branch)
+    grad_att = dot_nt(branch_rows, wo).astype(bf16)
+    grad_packed = exchange(pack_heads(grad_att, b, c), True, 3).reshape(8, 128, 128)
+    back = attend_back(valid[None], packed, grad_packed)
+
+    up_sum = fold(after(up_sum, grad_packed), flip_y, y, 2)
+    down_sum = fold(after(down_sum, grad_packed), flip_x, x, 2)
+    gw_out = contract_rows(attended, branch_rows).astype(bf16).reshape(2, 2, 2, 32, width)
+    back = exchange(back.reshape(2, 2, 2, 384, 128), False, 4)
+    grad_qk = back[:, :, :256].reshape(4, 2, 2, 128, 128).transpose(1, 2, 3, 0, 4).reshape(2, 2, 128, 512)
+    grad_qk = sort_ranks(grad_qk, b, c).reshape(512, 512)
+    grad_v = sort_ranks(unpack_heads(back[:, :, 256:]), b, c).reshape(512, 256)
+    gw_qk = contract_rows(first, grad_qk).astype(bf16).reshape(2, 2, 2, 2, 2, 32, 512)
+    gw_v = contract_rows(first, grad_v).astype(bf16).reshape(2, 2, 2, 2, 2, 32, 256)
+    _, pull_first = jax.vjp(norm_rows, hidden, gains[0], shifts[0])
+    part, gain1, shift1 = pull_first(scatter_rows(dot_nt(grad_qk, wqk) + dot_nt(grad_v, wv)))
+    input_grad = (grad_middle + part).astype(bf16)
+
+    out_sum = fold(fold(gw_out, flip_y, y, 1), flip_x, x, 2)
+    qk_sum = fold(fold(gw_qk, flip_x, x, 4), flip_y, y, 2)
+    v_sum = fold(fold(gw_v, flip_y, y, 2), flip_x, x, 4)
+    r_qk = fold_last(qk_sum, flip_a, a, 0).reshape(2, 2, 32, 512)
+    r_v = fold_last(v_sum, flip_a, a, 0).reshape(2, 2, 32, 256)
+    r_out = fold_last(out_sum, flip_a, a, 0).reshape(32, width)
+    r_up = fold_last(after(up_sum, back), flip_a, a, 0).reshape(2, 2, 32, 1024)
+    r_down = fold_last(after(down_sum, back), flip_a, a, 0).reshape(128, width)
+
+    def own_columns(block):
+        return sort_ranks(to_ranks(block, b, c), b, c)
+
+    r_qkv = own_columns(jnp.concatenate([r_qk, r_v], 3))
+    r_up = own_columns(r_up).reshape(2, 2, 32, 2, 2, 2, 128).transpose(2, 3, 0, 4, 1, 5, 6).reshape(32, 4096)
+    out_qk = r_qkv[..., :512].reshape(2, 2, 32, 2, 2, 2, HD).transpose(2, 5, 3, 0, 4, 1, 6).reshape(32, 2048)
+    out_v = r_qkv[..., 512:].reshape(2, 2, 32, 2, 2, HD).transpose(2, 3, 0, 4, 1, 5).reshape(32, 1024)
+
+    def in_ranks(block, axes):
+        for axis, flag in axes:
+            spots = lax.broadcasted_iota(jnp.int32, [2 if i == axis else 1 for i in range(block.ndim)], axis)
+            block = jnp.where(spots == flag, block, 0.0)
+        return block
+
+    def head_sums(block):
+        sums = jnp.sum(block.astype(f32), 0).reshape(2, 1, 2, 1, -1)[..., :HD]
+        sums = jnp.broadcast_to(sums, (2, 2, 2, 2, HD))
+        return in_ranks(sums, ((1, b), (3, c))).reshape(1, width)
+
+    whole = jnp.stack([
+        jnp.sum(grad_branch.astype(f32), 0), jnp.sum(grad_down.astype(f32), 0),
+        gain1, gain2, gain3, gain4, shift1, shift2, shift3, shift4])
+    vecs = jnp.concatenate([head_sums(grad_qk), head_sums(grad_v), whole], 0)
+    vecs = vecs.reshape(12, 32, 32).transpose(1, 0, 2).reshape(2, 2, 2, 2, 2, 3, 128)
+    sums_up = jnp.broadcast_to(jnp.sum(grad_up.astype(f32), 0).reshape(2, 1, 2, 1, 2, 1, 128), (2, 2, 2, 2, 2, 1, 128))
+    sums_up = in_ranks(sums_up, ((1, b), (3, c)))
+    terms = jnp.concatenate([vecs, sums_up, jnp.zeros((2, 2, 2, 2, 2, 4, 128), f32)], 5)
+    for flip_one, index, axis in ((flip_x, x, 4), (flip_y, y, 2), (flip_a, a, 0), (flip_b, b, 1), (flip_core, c, 3)):
+        terms = pick(terms, index, axis, True) + flip_one(pick(terms, 1 - index, axis, True))
+    small = terms.reshape(8, 128)
+    vectors = small[:3].reshape(12, 32)
+
+    return (
+        output[None], input_grad[None], jnp.concatenate([out_qk, out_v], 1), vectors[:2], r_out,
+        vectors[2], r_up, small[3], r_down, vectors[3], vectors[4:8], vectors[8:12])
+
+
 def solution(mesh):
     return jax.shard_map(
-        body,
+        fast_body if is_small(mesh) else body,
         mesh=mesh,
         in_specs=(
             P("dp", "seq", None),

time: 2260 us -> 419 us (0.19)
  waiting for transfers between devices: 1610 us -> 131 us
  blocking collectives: 345 us -> 0 us
  Pallas kernels: 0 us -> 81 us
  local copies, waits for them, and re-layouts: 129 us -> 60.1 us
  matrix products: 93.9 us -> 31.4 us
  starting transfers between devices: 0.86 us -> 62.5 us
  loops' own time: 27.1 us -> 0 us
    reduce_scatter x4 -> x0, waiting for transfers between devices: 1020 us -> none  [the longest x1 361 us: body(): lax.psum_scatter(grad_w_down, ('seq', 'dp'), scatter_dimension=0, tiled=T...]
    unnamed x20 -> x0, waiting for transfers between devices: 462 us -> none
    all_gather x4 -> x0, blocking collectives: 267 us -> none  [the longest x1 70.7 us: body(): lax.all_gather(norm_shift, ('seq', 'dp'), axis=1, tiled=True)]
    ppermute x0 -> x77, waiting for transfers between devices: none -> 131 us  [the longest x65 103 us: flip(): return lax.ppermute(block, 'seq', [(s, s ^ bits) for s in range(16)])]
    all_gather x6 -> x0, waiting for transfers between devices: 128 us -> none  [the longest x1 69 us: body(): lax.all_gather(w_down, ('seq', 'dp'), axis=0, tiled=True)]
    pallas_call x0 -> x8, Pallas kernels: none -> 81 us  [the longest x4 58.1 us: exchange(): pl.pallas_call(functools.partial(exchange_kernel, scatter), out_shape=jax...]
    unnamed x2 -> x0, blocking collectives: 78 us -> none
    ppermute x0 -> x77, starting transfers between devices: none -> 62.5 us  [the longest x65 45 us: flip(): return lax.ppermute(block, 'seq', [(s, s ^ bits) for s in range(16)])]
  transfers between devices with their start and end apart: 15 -> 77, of which waited for: 11 -> 38; matrix products, arithmetic and copies ran while one was open for 5% -> 20% of each run, Pallas kernels for 0% -> 9%
where the time goes in v1:
time: 419 us; the launch traced here: 412 us
  waiting for transfers between devices  131 us (31%)
  Pallas kernels  81 us (19%)
  starting transfers between devices  62.5 us (15%)
  local copies, waits for them, and re-layouts  60.1 us (14%)
  other arithmetic  41.2 us (10%)
  matrix products  31.4 us (7%)
  between operations  5.02 us (1%)
    ppermute x65, waiting for transfers between devices, flip(): return lax.ppermute(block, 'seq', [(s, s ^ bits) for s in range(16)])  103 us
    pallas_call x4, Pallas kernels, exchange(): pl.pallas_call(functools.partial(exchange_kernel, scatter), out_shape=jax...  58.1 us
    ppermute x65, starting transfers between devices, flip(): return lax.ppermute(block, 'seq', [(s, s ^ bits) for s in range(16)])  45 us
    ppermute x12, waiting for transfers between devices, flip_x(): return lax.ppermute(block, 'dp', [(0, 1), (1, 0)])  27.4 us
    ppermute x12, starting transfers between devices, flip_x(): return lax.ppermute(block, 'dp', [(0, 1), (1, 0)])  17.5 us
    dot_general x5, matrix products, dot_nn(): return jnp.dot(a, b, preferred_element_type=jnp.float32)  13.1 us
    pallas_call x1, Pallas kernels, attend_back(): pl.pallas_call(attend_back_kernel, out_shape=jax.ShapeDtypeStruct(packed....  11.6 us
    dot_general x5, matrix products, contract_rows(): lax.dot_general(left, right, (((0,), (0,)), ((), ())), preferred_element_...  9.37 us
  transfers between devices with their start and end apart: 77, of which 38 were waited for; matrix products, arithmetic and copies ran while one was open for 20% of the time, Pallas kernels for 9%

profile of v1, /device:TPU:0, one launch (start us, length us, event | category | flops | bytes accessed | tf_op | source)
XLA Modules:
  0.0 412.0 jit_solution(2111908631250103855)
XLA Ops:
  8.4 2.9 collective-permute-start.18
  51.8 5.7 %collective-permute-done.20 = bf16[4,32,1024]{2,1,0:T(8,128)(2,1)} collective-permute-done((bf16[4,32,1024]{2,1,0:T(8,128)(2,1)S(1)}, bf16[4,32,1024]{2,1,0:T(8,128)(2,1)}, u32[]{:S(2)}, u32[]{:S(2)}) %collective-permute-start.20) | collective-permute-done | bytes 262176 | tf_op jit(solution)/shard_map/ppermute | solution.py:457
  64.2 5.1 %collective-permute-done.14 = bf16[4,2,2,32,512]{4,3,2,1,0:T(8,128)(2,1)S(1)} collective-permute-done((bf16[4,2,2,32,512]{4,3,2,1,0:T(8,128)(2,1)S(1)}, bf16[4,2,2,32,512]{4,3,2,1,0:T(8,128)(2,1)S(1)}, u32[]{:S(2)}, u32[]{:S(2)}) %collective-permute-start.14) | collective-permute-done | bytes 524320 | tf_op jit(solution)/shard_map/ppermute | solution.py:464
  74.3 2.7 fusion.12
  79.6 16.9 %exchange.4 = bf16[2,2,2,384,128]{4,3,2,1,0:T(8,128)(2,1)} custom-call(bf16[4,2,384,128]{3,2,1,0:T(8,128)(2,1)} %pad_maximum_fusion.9.src), custom_call_target="tpu_custom_call" | custom-call | bytes 38400000 | tf_op jit(solution)/shard_map/exchange/pallas_call | solution.py:336
  97.6 8.0 %attend.1 = bf16[8,128,128]{2,1,0:T(8,128)(2,1)S(1)} custom-call(s32[1]{0:T(128)} %dynamic_slice.239.valid_ref, bf16[8,384,128]{2,1,0:T(8,128)(2,1)S(1)} %bitcast.308), custom_call_target="tpu_custom_call" | custom-call | tf_op jit(solution)/shard_map/attend/pallas_call | solution.py:432
  106.4 8.3 %exchange.5 = bf16[4,2,128,128]{3,2,1,0:T(8,128)(2,1)} custom-call(bf16[2,2,2,128,128]{4,3,2,1,0:T(8,128)(2,1)} %bitcast.314), custom_call_target="tpu_custom_call" | custom-call | bytes 12800000 | tf_op jit(solution)/shard_map/exchange/pallas_call | solution.py:336
  121.2 11.6 %collective-permute-done.30 = bf16[2,2,32,1024]{3,2,1,0:T(8,128)(2,1)S(1)} collective-permute-done((bf16[2,2,32,1024]{3,2,1,0:T(8,128)(2,1)S(1)}, bf16[2,2,32,1024]{3,2,1,0:T(8,128)(2,1)S(1)}, u32[]{:S(2)}, u32[]{:S(2)}) %collective-permute-start.30) | collective-permute-done | bytes 262176 | tf_op jit(solution)/shard_map/ppermute | solution.py:457
  139.5 8.4 %collective-permute-done.31 = bf16[2,2,2,32,1024]{4,3,2,1,0:T(8,128)(2,1)} collective-permute-done((bf16[2,2,2,32,1024]{4,3,2,1,0:T(8,128)(2,1)S(1)}, bf16[2,2,2,32,1024]{4,3,2,1,0:T(8,128)(2,1)}, u32[]{:S(2)}, u32[]{:S(2)}) %collective-permute-start.31) | collective-permute-done | bytes 524320 | tf_op jit(solution)/shard_map/ppermute | solution.py:457
  153.8 5.3 %collective-permute-done.25 = bf16[128,1024]{1,0:T(8,128)(2,1)S(1)} collective-permute-done((bf16[128,1024]{1,0:T(8,128)(2,1)S(1)}, bf16[128,1024]{1,0:T(8,128)(2,1)S(1)}, u32[]{:S(2)}, u32[]{:S(2)}) %collective-permute-start.25) | collective-permute-done | bytes 262176 | tf_op jit(solution)/shard_map/ppermute | solution.py:457
  159.1 10.2 %collective-permute-done.35 = bf16[4,128,1024]{2,1,0:T(8,128)(2,1)S(1)} collective-permute-done((bf16[4,128,1024]{2,1,0:T(8,128)(2,1)S(1)}, bf16[4,128,1024]{2,1,0:T(8,128)(2,1)S(1)}, u32[]{:S(2)}, u32[]{:S(2)}) %collective-permute-start.35) | collective-permute-done | bytes 1048608 | tf_op jit(solution)/shard_map/ppermute | solution.py:457
  169.5 2.9 collective-permute-done.32
  175.3 8.2 %multiply_convert_fusion = (bf16[512,1024]{1,0:T(8,128)(2,1)S(1)}, f32[512,1024]{1,0:T(8,128)}, f32[512,1024]{1,0:T(8,128)}) fusion(f32[1024]{0:T(1024)S(1)} %bitcast.396, bf16[1024,1024]{1,0:T(8,128)(2,1)S(1)} %bitcast.319, bf16[128,1024]{1,0:T(8,128)(2,1)S(1)} %collective-permute-done.26, bf16[128,1024]{1,0:T(8,128)(2,1)S(1)} %collective-permute-done.25, ...), kind=kOutput, calls=%fused_computation.16 | convolution fusion | flops 1112539136 | bytes 8392704 | tf_op jit(solution)/shard_map/dot_general | solution.py:351
  189.3 7.8 %collective-permute-done.38 = bf16[128,1024]{1,0:T(8,128)(2,1)} collective-permute-done((bf16[128,1024]{1,0:T(8,128)(2,1)}, bf16[128,1024]{1,0:T(8,128)(2,1)}, u32[]{:S(2)}, u32[]{:S(2)}) %collective-permute-start.38) | collective-permute-done | bytes 262176 | tf_op jit(solution)/shard_map/ppermute | solution.py:457
  200.6 7.2 %collective-permute-done.40 = bf16[128,1024]{1,0:T(8,128)(2,1)S(1)} collective-permute-done((bf16[128,1024]{1,0:T(8,128)(2,1)S(1)}, bf16[128,1024]{1,0:T(8,128)(2,1)S(1)}, u32[]{:S(2)}, u32[]{:S(2)}) %collective-permute-start.40) | collective-permute-done | bytes 262176 | tf_op jit(solution)/shard_map/ppermute | solution.py:457
  209.4 3.7 convert_reduce_fusion.1
  217.9 2.9 convolution_convert_fusion.1
  229.2 4.0 collective-permute-done.44
  242.2 5.3 %collective-permute-done.68 = bf16[2,2,2,2,1,32,1024]{6,5,4,3,2,1,0:T(8,128)(2,1)} collective-permute-done((bf16[2,2,2,2,1,32,1024]{6,5,4,3,2,1,0:T(8,128)(2,1)}, bf16[2,2,2,2,1,32,1024]{6,5,4,3,2,1,0:T(8,128)(2,1)}, u32[]{:S(2)}, u32[]{:S(2)}) %collective-permute-start.68) | collective-permute-done | bytes 1048608 | tf_op jit(solution)/shard_map/ppermute | solution.py:464
  247.5 3.0 add_convert_fusion.1
  262.7 11.5 %exchange.6 = bf16[2,2,2,128,128]{4,3,2,1,0:T(8,128)(2,1)} custom-call(bf16[4,2,128,128]{3,2,1,0:T(8,128)(2,1)} %copy.87.src), custom_call_target="tpu_custom_call" | custom-call | bytes 12800000 | tf_op jit(solution)/shard_map/exchange/pallas_call | solution.py:336
  275.2 11.6 %attend_back.1 = bf16[8,384,128]{2,1,0:T(8,128)(2,1)S(1)} custom-call(s32[1]{0:T(128)} %dynamic_slice.239.valid_ref, bf16[8,384,128]{2,1,0:T(8,128)(2,1)S(1)} %bitcast.309, bf16[8,128,128]{2,1,0:T(8,128)(2,1)S(1)} %bitcast.313), custom_call_target="tpu_custom_call" | custom-call | tf_op jit(solution)/shard_map/attend_back/pallas_call | solution.py:445
  287.7 21.3 %exchange.7 = bf16[4,2,384,128]{3,2,1,0:T(8,128)(2,1)} custom-call(bf16[2,2,2,384,128]{4,3,2,1,0:T(8,128)(2,1)} %bitcast.310), custom_call_target="tpu_custom_call" | custom-call | bytes 38400000 | tf_op jit(solution)/shard_map/exchange/pallas_call | solution.py:336
  312.7 3.0 convolution_convert_fusion.2
  332.6 3.8 collective-permute-done.54
  339.0 5.2 %collective-permute-done.66 = bf16[2,1,1,32,1024]{4,3,2,1,0:T(8,128)(2,1)S(1)} collective-permute-done((bf16[2,1,1,32,1024]{4,3,2,1,0:T(8,128)(2,1)S(1)}, bf16[2,1,1,32,1024]{4,3,2,1,0:T(8,128)(2,1)S(1)}, u32[]{:S(2)}, u32[]{:S(2)}) %collective-permute-start.66) | collective-permute-done | bytes 131104 | tf_op jit(solution)/shard_map/ppermute | solution.py:464
  345.7 3.4 collective-permute-done.55
  349.2 6.3 %collective-permute-done.67 = bf16[1,1,1,32,1024]{4,3,2,1,0:T(8,128)(2,1)S(1)} collective-permute-done((bf16[1,1,1,32,1024]{4,3,2,1,0:T(8,128)(2,1)S(1)}, bf16[1,1,1,32,1024]{4,3,2,1,0:T(8,128)(2,1)S(1)}, u32[]{:S(2)}, u32[]{:S(2)}) %collective-permute-start.67) | collective-permute-done | bytes 65568 | tf_op jit(solution)/shard_map/ppermute | solution.py:457
  356.2 4.5 %collective-permute-done.56 = bf16[1,2,1,2,1,32,256]{6,5,3,1,4,2,0:T(8,128)(2,1)S(1)} collective-permute-done((bf16[1,2,1,2,1,32,256]{6,5,3,1,4,2,0:T(8,128)(2,1)S(1)}, bf16[1,2,1,2,1,32,256]{6,5,3,1,4,2,0:T(8,128)(2,1)S(1)}, u32[]{:S(2)}, u32[]{:S(2)}) %collective-permute-start.56) | collective-permute-done | bytes 65568 | tf_op jit(solution)/shard_map/ppermute | solution.py:457
  364.6 2.8 collective-permute-start.70
  371.0 2.9 collective-permute-start.53
  388.7 3.6 collective-permute-done.62
  (539 shorter events, 197.2 us)
Async XLA Ops:
  8.3 41.6 %collective-permute-start.1 = (bf16[128,1024]{1,0:T(8,128)(2,1)}, bf16[128,1024]{1,0:T(8,128)(2,1)S(1)}, u32[]{:S(2)}, u32[]{:S(2)}) collective-permute-start(bf16[128,1024]{1,0:T(8,128)(2,1)} %bitcast.323), channel_id=1, source_target_pairs={{0,8},{2,10},{4,12},{6,14},{8,0},{10,2},{12,4},{14,6},{16,24},{18,... | collective-permute-start | bytes 786440 | tf_op jit(solution)/shard_map/ppermute | solution.py:457
  8.3 54.7 %collective-permute-start = (bf16[128,1024]{1,0:T(8,128)(2,1)}, bf16[128,1024]{1,0:T(8,128)(2,1)S(1)}, u32[]{:S(2)}, u32[]{:S(2)}) collective-permute-start(bf16[128,1024]{1,0:T(8,128)(2,1)} %bitcast.324), channel_id=1, source_target_pairs={{0,2},{2,0},{4,6},{6,4},{8,10},{10,8},{12,14},{14,12},{16,18},{18,... | collective-permute-start | bytes 786440 | tf_op jit(solution)/shard_map/ppermute | solution.py:457
  8.4 21.8 %collective-permute-start.18 = (bf16[32,1024]{1,0:T(8,128)(2,1)}, bf16[32,1024]{1,0:T(8,128)(2,1)S(1)}, u32[]{:S(2)}, u32[]{:S(2)}) collective-permute-start(bf16[32,1024]{1,0:T(8,128)(2,1)} %param.20), channel_id=1, source_target_pairs={{0,16},{2,18},{4,20},{6,22},{8,24},{10,26},{12,28},{14,30},{16,0},... | collective-permute-start | bytes 196616 | tf_op jit(solution)/shard_map/ppermute | solution.py:457
  44.8 12.7 %collective-permute-start.20 = (bf16[4,32,1024]{2,1,0:T(8,128)(2,1)S(1)}, bf16[4,32,1024]{2,1,0:T(8,128)(2,1)}, u32[]{:S(2)}, u32[]{:S(2)}) collective-permute-start(bf16[4,32,1024]{2,1,0:T(8,128)(2,1)S(1)} %pad_maximum_fusion.20), channel_id=1, source_target_pairs={{0,4},{2,6},{4,0},{6,2},{8,12},{10,14},{12,8},{14,10},{16,20},{18,... | collective-permute-start | bytes 786440 | tf_op jit(solution)/shard_map/ppermute | solution.py:457
  46.4 15.6 %collective-permute-start.17 = (bf16[4,2,2,32,256]{4,3,2,1,0:T(8,128)(2,1)S(1)}, bf16[4,2,2,32,256]{4,3,2,1,0:T(8,128)(2,1)}, u32[]{:S(2)}, u32[]{:S(2)}) collective-permute-start(bf16[4,2,2,32,256]{4,3,2,1,0:T(8,128)(2,1)S(1)} %pad_maximum_fusion.19), channel_id=1, source_target_pairs={{0,4},{2,6},{4,0},{6,2},{8,12},{10,14},{12,8},{14,10},{16,20},{18,... | collective-permute-start | bytes 786440 | tf_op jit(solution)/shard_map/ppermute | solution.py:457
  49.8 68.8 %collective-permute-start.33 = (bf16[128,1024]{1,0:T(8,128)(2,1)}, bf16[128,1024]{1,0:T(8,128)(2,1)}, u32[]{:S(2)}, u32[]{:S(2)}) collective-permute-start(bf16[128,1024]{1,0:T(8,128)(2,1)} %param.24), channel_id=1, source_target_pairs={{0,16},{2,18},{4,20},{6,22},{8,24},{10,26},{12,28},{14,30},{16,0},... | collective-permute-start | bytes 786440 | tf_op jit(solution)/shard_map/ppermute | solution.py:457
  51.7 11.3 %collective-permute-start.2 = (bf16[128,1024]{1,0:T(8,128)(2,1)S(1)}, bf16[128,1024]{1,0:T(8,128)(2,1)S(1)}, u32[]{:S(2)}, u32[]{:S(2)}) collective-permute-start(bf16[128,1024]{1,0:T(8,128)(2,1)S(1)} %collective-permute-done.1), channel_id=1, source_target_pairs={{0,2},{2,0},{4,6},{6,4},{8,10},{10,8},{12,14},{14,12},{16,18},{18,... | collective-permute-start | bytes 786440 | tf_op jit(solution)/shard_map/ppermute | solution.py:457
  57.5 11.9 %collective-permute-start.14 = (bf16[4,2,2,32,512]{4,3,2,1,0:T(8,128)(2,1)S(1)}, bf16[4,2,2,32,512]{4,3,2,1,0:T(8,128)(2,1)S(1)}, u32[]{:S(2)}, u32[]{:S(2)}) collective-permute-start(bf16[4,2,2,32,512]{4,3,2,1,0:T(8,128)(2,1)S(1)} %pad_maximum_fusion.10), channel_id=1, source_target_pairs={{0,1},{1,0},{2,3},{3,2},{4,5},{5,4},{6,7},{7,6},{8,9},{9,8},{10,11... | collective-permute-start | bytes 1572872 | tf_op jit(solution)/shard_map/ppermute | solution.py:464
  117.7 18.4 %collective-permute-start.22 = (f32[128,1024]{1,0:T(8,128)}, f32[128,1024]{1,0:T(8,128)}, u32[]{:S(2)}, u32[]{:S(2)}) collective-permute-start(f32[128,1024]{1,0:T(8,128)} %get-tuple-element.100), channel_id=1, source_target_pairs={{0,2},{2,0},{4,6},{6,4},{8,10},{10,8},{12,14},{14,12},{16,18},{18,... | collective-permute-start | bytes 1572872 | tf_op jit(solution)/shard_map/ppermute | solution.py:457
  117.8 15.0 %collective-permute-start.30 = (bf16[2,2,32,1024]{3,2,1,0:T(8,128)(2,1)S(1)}, bf16[2,2,32,1024]{3,2,1,0:T(8,128)(2,1)S(1)}, u32[]{:S(2)}, u32[]{:S(2)}) collective-permute-start(bf16[2,2,32,1024]{3,2,1,0:T(8,128)(2,1)S(1)} %reverse_select_fusion.10), channel_id=1, source_target_pairs={{0,16},{2,18},{4,20},{6,22},{8,24},{10,26},{12,28},{14,30},{16,0},... | collective-permute-start | bytes 786440 | tf_op jit(solution)/shard_map/ppermute | solution.py:457
  119.7 17.8 %collective-permute-start.34 = (bf16[2,128,1024]{2,1,0:T(8,128)(2,1)S(1)}, bf16[2,128,1024]{2,1,0:T(8,128)(2,1)}, u32[]{:S(2)}, u32[]{:S(2)}) collective-permute-start(bf16[2,128,1024]{2,1,0:T(8,128)(2,1)S(1)} %pad_maximum_fusion.14), channel_id=1, source_target_pairs={{0,1},{1,0},{2,3},{3,2},{4,5},{5,4},{6,7},{7,6},{8,9},{9,8},{10,11... | collective-permute-start | bytes 1572872 | tf_op jit(solution)/shard_map/ppermute | solution.py:464
  132.9 15.0 %collective-permute-start.31 = (bf16[2,2,2,32,1024]{4,3,2,1,0:T(8,128)(2,1)S(1)}, bf16[2,2,2,32,1024]{4,3,2,1,0:T(8,128)(2,1)}, u32[]{:S(2)}, u32[]{:S(2)}) collective-permute-start(bf16[2,2,2,32,1024]{4,3,2,1,0:T(8,128)(2,1)S(1)} %pad_maximum_fusion.13), channel_id=1, source_target_pairs={{0,4},{2,6},{4,0},{6,2},{8,12},{10,14},{12,8},{14,10},{16,20},{18,... | collective-permute-start | bytes 1572872 | tf_op jit(solution)/shard_map/ppermute | solution.py:457
  136.1 14.4 %collective-permute-start.21 = (f32[128,1024]{1,0:T(8,128)}, f32[128,1024]{1,0:T(8,128)S(1)}, u32[]{:S(2)}, u32[]{:S(2)}) collective-permute-start(f32[128,1024]{1,0:T(8,128)} %get-tuple-element.99), channel_id=1, source_target_pairs={{0,2},{2,0},{4,6},{6,4},{8,10},{10,8},{12,14},{14,12},{16,18},{18,... | collective-permute-start | bytes 1572872 | tf_op jit(solution)/shard_map/ppermute | solution.py:457
  137.4 13.1 %collective-permute-start.23 = (bf16[128,1024]{1,0:T(8,128)(2,1)S(1)}, bf16[128,1024]{1,0:T(8,128)(2,1)S(1)}, u32[]{:S(2)}, u32[]{:S(2)}) collective-permute-start(bf16[128,1024]{1,0:T(8,128)(2,1)S(1)} %fusion.36), channel_id=1, source_target_pairs={{0,8},{2,10},{4,12},{6,14},{8,0},{10,2},{12,4},{14,6},{16,24},{18,... | collective-permute-start | bytes 786440 | tf_op jit(solution)/shard_map/ppermute | solution.py:457
  138.6 30.7 %collective-permute-start.35 = (bf16[4,128,1024]{2,1,0:T(8,128)(2,1)S(1)}, bf16[4,128,1024]{2,1,0:T(8,128)(2,1)S(1)}, u32[]{:S(2)}, u32[]{:S(2)}) collective-permute-start(bf16[4,128,1024]{2,1,0:T(8,128)(2,1)S(1)} %pad_maximum_fusion.6), channel_id=1, source_target_pairs={{0,4},{2,6},{4,0},{6,2},{8,12},{10,14},{12,8},{14,10},{16,20},{18,... | collective-permute-start | bytes 3145736 | tf_op jit(solution)/shard_map/ppermute | solution.py:457
  149.0 23.5 %collective-permute-start.32 = (bf16[4,2,2,32,1024]{4,3,2,1,0:T(8,128)(2,1)S(1)}, bf16[4,2,2,32,1024]{4,3,2,1,0:T(8,128)(2,1)S(1)}, u32[]{:S(2)}, u32[]{:S(2)}) collective-permute-start(bf16[4,2,2,32,1024]{4,3,2,1,0:T(8,128)(2,1)S(1)} %pad_maximum_fusion.5), channel_id=1, source_target_pairs={{0,1},{1,0},{2,3},{3,2},{4,5},{5,4},{6,7},{7,6},{8,9},{9,8},{10,11... | collective-permute-start | bytes 3145736 | tf_op jit(solution)/shard_map/ppermute | solution.py:464
  153.8 21.5 %collective-permute-start.24 = (bf16[128,1024]{1,0:T(8,128)(2,1)S(1)}, bf16[128,1024]{1,0:T(8,128)(2,1)S(1)}, u32[]{:S(2)}, u32[]{:S(2)}) collective-permute-start(bf16[128,1024]{1,0:T(8,128)(2,1)S(1)} %add_convert_fusion.13), channel_id=1, source_target_pairs={{0,2},{2,0},{4,6},{6,4},{8,10},{10,8},{12,14},{14,12},{16,18},{18,... | collective-permute-start | bytes 786440 | tf_op jit(solution)/shard_map/ppermute | solution.py:457
  159.1 16.1 %collective-permute-start.26 = (bf16[128,1024]{1,0:T(8,128)(2,1)S(1)}, bf16[128,1024]{1,0:T(8,128)(2,1)S(1)}, u32[]{:S(2)}, u32[]{:S(2)}) collective-permute-start(bf16[128,1024]{1,0:T(8,128)(2,1)S(1)} %collective-permute-done.25), channel_id=1, source_target_pairs={{0,2},{2,0},{4,6},{6,4},{8,10},{10,8},{12,14},{14,12},{16,18},{18,... | collective-permute-start | bytes 786440 | tf_op jit(solution)/shard_map/ppermute | solution.py:457
  217.6 11.6 %collective-permute-start.42 = (f32[128,1024]{1,0:T(8,128)}, f32[128,1024]{1,0:T(8,128)S(1)}, u32[]{:S(2)}, u32[]{:S(2)}) collective-permute-start(f32[128,1024]{1,0:T(8,128)} %get-tuple-element.95), channel_id=1, source_target_pairs={{0,2},{2,0},{4,6},{6,4},{8,10},{10,8},{12,14},{14,12},{16,18},{18,... | collective-permute-start | bytes 1572872 | tf_op jit(solution)/shard_map/ppermute | solution.py:457
  222.0 25.5 %collective-permute-start.68 = (bf16[2,2,2,2,1,32,1024]{6,5,4,3,2,1,0:T(8,128)(2,1)}, bf16[2,2,2,2,1,32,1024]{6,5,4,3,2,1,0:T(8,128)(2,1)}, u32[]{:S(2)}, u32[]{:S(2)}) collective-permute-start(bf16[2,2,2,2,1,32,1024]{6,5,4,3,2,1,0:T(8,128)(2,1)} %constant_dynamic-slice_fusion.6), channel_id=1, source_target_pairs={{0,1},{1,0},{2,3},{3,2},{4,5},{5,4},{6,7},{7,6},{8,9},{9,8},{10,11... | collective-permute-start | bytes 3145736 | tf_op jit(solution)/shard_map/ppermute | solution.py:464
  227.9 25.2 %collective-permute-start.74 = (bf16[2,1,2,128,1024]{4,3,2,1,0:T(8,128)(2,1)}, bf16[2,1,2,128,1024]{4,3,2,1,0:T(8,128)(2,1)}, u32[]{:S(2)}, u32[]{:S(2)}) collective-permute-start(bf16[2,1,2,128,1024]{4,3,2,1,0:T(8,128)(2,1)} %constant_dynamic-slice_fusion.3), channel_id=1, source_target_pairs={{0,4},{2,6},{4,0},{6,2},{8,12},{10,14},{12,8},{14,10},{16,20},{18,... | collective-permute-start | bytes 3145736 | tf_op jit(solution)/shard_map/ppermute | solution.py:457
  237.9 17.8 %collective-permute-start.45 = (bf16[128,1024]{1,0:T(8,128)(2,1)S(1)}, bf16[128,1024]{1,0:T(8,128)(2,1)S(1)}, u32[]{:S(2)}, u32[]{:S(2)}) collective-permute-start(bf16[128,1024]{1,0:T(8,128)(2,1)S(1)} %get-tuple-element.71), channel_id=1, source_target_pairs={{0,2},{2,0},{4,6},{6,4},{8,10},{10,8},{12,14},{14,12},{16,18},{18,... | collective-permute-start | bytes 786440 | tf_op jit(solution)/shard_map/ppermute | solution.py:457
  242.2 13.5 %collective-permute-start.47 = (bf16[128,1024]{1,0:T(8,128)(2,1)S(1)}, bf16[128,1024]{1,0:T(8,128)(2,1)S(1)}, u32[]{:S(2)}, u32[]{:S(2)}) collective-permute-start(bf16[128,1024]{1,0:T(8,128)(2,1)S(1)} %collective-permute-done.46), channel_id=1, source_target_pairs={{0,2},{2,0},{4,6},{6,4},{8,10},{10,8},{12,14},{14,12},{16,18},{18,... | collective-permute-start | bytes 786440 | tf_op jit(solution)/shard_map/ppermute | solution.py:457
  323.4 13.0 %collective-permute-start.54 = (bf16[2,2,1,2,2,32,256]{6,5,3,1,4,2,0:T(8,128)(2,1)}, bf16[2,2,1,2,2,32,256]{6,5,3,1,4,2,0:T(8,128)(2,1)}, u32[]{:S(2)}, u32[]{:S(2)}) collective-permute-start(bf16[2,2,1,2,2,32,256]{6,5,3,1,4,2,0:T(8,128)(2,1)} %copy.107), channel_id=1, source_target_pairs={{0,4},{2,6},{4,0},{6,2},{8,12},{10,14},{12,8},{14,10},{16,20},{18,... | collective-permute-start | bytes 786440 | tf_op jit(solution)/shard_map/ppermute | solution.py:457
  328.0 34.3 %collective-permute-start.51 = (bf16[2,2,2,2,1,32,512]{6,5,3,1,4,2,0:T(8,128)(2,1)S(1)}, bf16[2,2,2,2,1,32,512]{6,5,3,1,4,2,0:T(8,128)(2,1)S(1)}, u32[]{:S(2)}, u32[]{:S(2)}) collective-permute-start(bf16[2,2,2,2,1,32,512]{6,5,3,1,4,2,0:T(8,128)(2,1)S(1)} %copy.105), channel_id=1, source_target_pairs={{0,1},{1,0},{2,3},{3,2},{4,5},{5,4},{6,7},{7,6},{8,9},{9,8},{10,11... | collective-permute-start | bytes 1572872 | tf_op jit(solution)/shard_map/ppermute | solution.py:464
  329.6 44.3 %collective-permute-start.48 = (f32[128,1024]{1,0:T(8,128)S(1)}, f32[128,1024]{1,0:T(8,128)S(1)}, u32[]{:S(2)}, u32[]{:S(2)}) collective-permute-start(f32[128,1024]{1,0:T(8,128)S(1)} %get-tuple-element.93), channel_id=1, source_target_pairs={{0,2},{2,0},{4,6},{6,4},{8,10},{10,8},{12,14},{14,12},{16,18},{18,... | collective-permute-start | bytes 1572872 | tf_op jit(solution)/shard_map/ppermute | solution.py:457
  329.7 33.7 %collective-permute-start.49 = (f32[128,1024]{1,0:T(8,128)S(1)}, f32[128,1024]{1,0:T(8,128)S(1)}, u32[]{:S(2)}, u32[]{:S(2)}) collective-permute-start(f32[128,1024]{1,0:T(8,128)S(1)} %get-tuple-element.94), channel_id=1, source_target_pairs={{0,2},{2,0},{4,6},{6,4},{8,10},{10,8},{12,14},{14,12},{16,18},{18,... | collective-permute-start | bytes 1572872 | tf_op jit(solution)/shard_map/ppermute | solution.py:457
  330.8 32.8 %collective-permute-start.69 = (bf16[2,2,1,2,1,32,1024]{6,5,4,3,2,1,0:T(8,128)(2,1)S(1)}, bf16[2,2,1,2,1,32,1024]{6,5,4,3,2,1,0:T(8,128)(2,1)S(1)}, u32[]{:S(2)}, u32[]{:S(2)}) collective-permute-start(bf16[2,2,1,2,1,32,1024]{6,5,4,3,2,1,0:T(8,128)(2,1)S(1)} %constant_dynamic-slice_fusion.5), channel_id=1, source_target_pairs={{0,4},{2,6},{4,0},{6,2},{8,12},{10,14},{12,8},{14,10},{16,20},{18,... | collective-permute-start | bytes 1572872 | tf_op jit(solution)/shard_map/ppermute | solution.py:457
  364.6 23.2 %collective-permute-start.70 = (bf16[1,2,1,2,1,32,1024]{6,5,4,3,2,1,0:T(8,128)(2,1)}, bf16[1,2,1,2,1,32,1024]{6,5,4,3,2,1,0:T(8,128)(2,1)}, u32[]{:S(2)}, u32[]{:S(2)}) collective-permute-start(bf16[1,2,1,2,1,32,1024]{6,5,4,3,2,1,0:T(8,128)(2,1)} %constant_dynamic-slice_fusion.4), channel_id=1, source_target_pairs={{0,16},{2,18},{4,20},{6,22},{8,24},{10,26},{12,28},{14,30},{16,0},... | collective-permute-start | bytes 786440 | tf_op jit(solution)/shard_map/ppermute | solution.py:457
  370.2 25.9 %collective-permute-start.76 = (bf16[1,1,1,128,1024]{4,3,2,1,0:T(8,128)(2,1)S(1)}, bf16[1,1,1,128,1024]{4,3,2,1,0:T(8,128)(2,1)}, u32[]{:S(2)}, u32[]{:S(2)}) collective-permute-start(bf16[1,1,1,128,1024]{4,3,2,1,0:T(8,128)(2,1)S(1)} %constant_dynamic-slice_fusion.1), channel_id=1, source_target_pairs={{0,16},{2,18},{4,20},{6,22},{8,24},{10,26},{12,28},{14,30},{16,0},... | collective-permute-start | bytes 786440 | tf_op jit(solution)/shard_map/ppermute | solution.py:457
  371.0 30.4 %collective-permute-start.53 = (bf16[1,2,1,2,1,32,512]{6,5,3,1,4,2,0:T(8,128)(2,1)}, bf16[1,2,1,2,1,32,512]{6,5,3,1,4,2,0:T(8,128)(2,1)S(1)}, u32[]{:S(2)}, u32[]{:S(2)}) collective-permute-start(bf16[1,2,1,2,1,32,512]{6,5,3,1,4,2,0:T(8,128)(2,1)} %constant_dynamic-slice_fusion.21), channel_id=1, source_target_pairs={{0,16},{2,18},{4,20},{6,22},{8,24},{10,26},{12,28},{14,30},{16,0},... | collective-permute-start | bytes 393224 | tf_op jit(solution)/shard_map/ppermute | solution.py:457
  392.5 11.0 %collective-permute-start.72 = (f32[32,1024]{1,0:T(8,128)S(1)}, f32[32,1024]{1,0:T(8,128)S(1)}, u32[]{:S(2)}, u32[]{:S(2)}) collective-permute-start(f32[32,1024]{1,0:T(8,128)S(1)} %get-tuple-element.106), channel_id=1, source_target_pairs={{0,8},{2,10},{4,12},{6,14},{8,0},{10,2},{12,4},{14,6},{16,24},{18,... | collective-permute-start | bytes 393224 | tf_op jit(solution)/shard_map/ppermute | solution.py:457
  (113 other events, 771.1 us)

commit v2 on v1

--- a/solution.py
+++ b/solution.py
@@ -561,9 +561,173 @@
     return add_low(pick(terms, index, axis, True), flip_one(pick(terms, 1 - index, axis, True)))
 
 
-def fold_last(terms, flip_one, index, axis):
-    return (pick(terms, index, axis, True).astype(jnp.float32)
-            + flip_one(pick(terms, 1 - index, axis, True)).astype(jnp.float32))
+def reduce_kernel(q_ref, o_ref, u_ref, d_ref, s_ref, rq, ro, ru, rd, rs,
+                  r1q, t2q, r2q, t3q, r3q, fq, gq, r1o, t2o, r2o, t3o, r3o, r3u, fu, gu, r3d,
+                  sx, s1, sy, s2, sa, s3, sb, s4, sc, send_sem, recv_sem):
+    a, b, y, c, x = place()
+    f32, bf16 = jnp.float32, jnp.bfloat16
+    barrier = pltpu.get_barrier_semaphore()
+
+    def at(pa, pb, py, pc, px):
+        return (pa * 8 + pb * 4 + py * 2 + pc, px)
+
+    to_x, to_y, to_a = at(a, b, y, c, 1 - x), at(a, b, 1 - y, c, x), at(1 - a, b, y, c, x)
+    ranks = [(lax.rem(b + k // 2, 2), lax.rem(c + k % 2, 2)) for k in range(4)]
+    to_rank = [at(a, ranks[k][0], y, ranks[k][1], x) for k in range(4)]
+    to_b, to_c = to_rank[2], to_rank[1]
+    for dev in [to_x, to_y, to_a] + to_rank[1:]:
+        pl.semaphore_signal(barrier, inc=1, device_id=dev, device_id_type=MESH)
+    pl.semaphore_wait(barrier, 6)
+
+    made = []
+
+    def remote(src, dst, dev):
+        k = len(made)
+        made.append(pltpu.make_async_remote_copy(
+            src_ref=src, dst_ref=dst, send_sem=send_sem.at[k], recv_sem=recv_sem.at[k],
+            device_id=dev, device_id_type=MESH))
+        return made[-1]
+
+    def low(*values):
+        return sum(v.astype(f32) for v in values)
+
+    places = [1 - a, a]
+    halves = [slice(0, 512), slice(512, 1024)]
+    lateral = [(to_x, to_y), (to_y, to_x)]
+
+    cu = remote(u_ref.at[1 - a], r3u, to_a)
+    cd = remote(d_ref.at[1 - a], r3d, to_a)
+    q1, q2, o1, o2 = {}, {}, {}, {}
+    for i in range(2):
+        for s in range(2):
+            p = places[i]
+            q1[s, i] = remote(q_ref.at[p, 0, :, :, 1 - x] if s == 0 else q_ref.at[p, 1, 1 - y], r1q.at[s, i], lateral[s][0])
+            o1[s, i] = remote(o_ref.at[p, :, 1 - x, :, halves[0]] if s == 0 else o_ref.at[p, 1 - y, :, :, halves[1]],
+                              r1o.at[s, i], lateral[s][0])
+            q2[s, i] = remote(t2q.at[s, i], r2q.at[s, i], lateral[s][1])
+            o2[s, i] = remote(t2o.at[s, i], r2o.at[s, i], lateral[s][1])
+    q3 = [remote(t3q.at[s], r3q.at[s], to_a) for s in range(2)]
+    o3 = [remote(t3o.at[s], r3o.at[s], to_a) for s in range(2)]
+    qr = [remote(fq.at[ranks[k][0], ranks[k][1]], gq.at[k - 1], to_rank[k]) for k in range(1, 4)]
+    ur = [remote(fu.at[ranks[k][0], ranks[k][1]], gu.at[k - 1], to_rank[k]) for k in range(1, 4)]
+    vx = remote(s_ref.at[:, :, :, :, 1 - x], sx, to_x)
+    vy = remote(s1.at[:, :, 1 - y], sy, to_y)
+    va = remote(s2.at[1 - a], sa, to_a)
+    vb = remote(s3.at[1 - b], sb, to_b)
+    vc = remote(s4.at[1 - c], sc, to_c)
+
+    cu.start()
+    vx.start()
+    for i in range(2):
+        for s in range(2):
+            q1[s, i].start()
+            o1[s, i].start()
+    cd.start()
+
+    def q_terms(s, i, far):
+        p = places[i]
+        if s == 0:
+            v = 1 - y if far else y
+            return q_ref[p, 0, v, :, x], r1q[0, i, v]
+        v = 1 - x if far else x
+        return q_ref[p, 1, y, :, v], r1q[1, i, :, v]
+
+    def o_terms(s, i, far):
+        p = places[i]
+        if s == 0:
+            v = 1 - y if far else y
+            return o_ref[p, v, x, :, halves[0]], r1o[0, i, v]
+        v = 1 - x if far else x
+        return o_ref[p, y, v, :, halves[1]], r1o[1, i, v]
+
+    for i in range(2):
+        for s in range(2):
+            q1[s, i].wait_recv()
+            t2q[s, i] = low(*q_terms(s, i, True)).astype(bf16)
+            q2[s, i].start()
+            o1[s, i].wait_recv()
+            t2o[s, i] = low(*o_terms(s, i, True)).astype(bf16)
+            o2[s, i].start()
+        if i == 0:
+            vx.wait_recv()
+            s1[...] = s_ref[:, :, :, :, x] + sx[...]
+            vy.start()
+            for s in range(2):
+                q2[s, 0].wait_recv()
+                t3q[s] = low(*q_terms(s, 0, False), r2q[s, 0]).astype(bf16)
+                q3[s].start()
+                o2[s, 0].wait_recv()
+                t3o[s] = low(*o_terms(s, 0, False), r2o[s, 0]).astype(bf16)
+                o3[s].start()
+    vy.wait_recv()
+    s2[...] = s1[:, :, y] + sy[...]
+    va.start()
+
+    cu.wait_recv()
+    for k in range(1, 4):
+        pb, pc = ranks[k]
+        fu[pb, pc] = low(u_ref[a, pb, pc], r3u[pb, pc]).astype(bf16)
+        ur[k - 1].start()
+    ru[b, c] = low(u_ref[a, b, c], r3u[b, c])
+
+    for s in range(2):
+        q2[s, 1].wait_recv()
+        o2[s, 1].wait_recv()
+        q3[s].wait_recv()
+        total = low(*q_terms(s, 1, False), r2q[s, 1], r3q[s])
+        fq[s] = total.astype(bf16)
+        for j in range(2):
+            @pl.when((b == s) & (c == j))
+            def _():
+                rq[s, j] = total[j]
+        o3[s].wait_recv()
+        ro[:, halves[s]] = low(*o_terms(s, 1, False), r2o[s, 1], r3o[s])
+    for k in (3, 2, 1):
+        qr[k - 1].start()
+    va.wait_recv()
+    s3[...] = s2[a] + sa[...]
+    vb.start()
+    cd.wait_recv()
+    rd[...] = low(d_ref[a], r3d[...])
+    vb.wait_recv()
+    s4[...] = s3[b] + sb[...]
+    vc.start()
+    for k in (1, 2, 3):
+        pb, pc = ranks[k]
+        ur[k - 1].wait_recv()
+        ru[pb, pc] = gu[k - 1].astype(f32)
+    for k in (1, 2, 3):
+        pb, pc = ranks[k]
+        qr[k - 1].wait_recv()
+        rq[pb, pc] = gq[k - 1].astype(f32)
+    vc.wait_recv()
+    rs[...] = s4[c] + sc[...]
+    for copy in made:
+        copy.wait_send()
+
+
+def reduce_all(gw_qkv, gw_out, up_sum, down_sum, small, cid):
+    f32, bf16 = jnp.float32, jnp.bfloat16
+    V = pltpu.VMEM
+    vm = pl.BlockSpec(memory_space=V)
+    S = jax.ShapeDtypeStruct
+    q, o = gw_qkv.shape[5:], (gw_out.shape[3], 512)
+    u, d, s = up_sum.shape[1:], down_sum.shape[1:], small.shape[5:]
+    scratch = [
+        V((2, 2, 2, 2) + q, bf16), V((2, 2, 2) + q, bf16), V((2, 2, 2) + q, bf16), V((2, 2) + q, bf16), V((2, 2) + q, bf16),
+        V((2, 2) + q, bf16), V((3,) + q, bf16),
+        V((2, 2, 2) + o, bf16), V((2, 2) + o, bf16), V((2, 2) + o, bf16), V((2,) + o, bf16), V((2,) + o, bf16),
+        V(u, bf16), V(u, bf16), V((3,) + u[2:], bf16), V(d, bf16),
+        V((2, 2, 2, 2) + s, f32), V((2, 2, 2, 2) + s, f32), V((2, 2, 2) + s, f32), V((2, 2, 2) + s, f32), V((2, 2) + s, f32),
+        V((2, 2) + s, f32), V((2,) + s, f32), V((2,) + s, f32), V(s, f32),
+        pltpu.SemaphoreType.DMA((33,)), pltpu.SemaphoreType.DMA((33,))]
+    return pl.pallas_call(
+        reduce_kernel,
+        out_shape=(S((2, 2) + q, f32), S((o[0], 1024), f32), S(u, f32), S(d, f32), S(s, f32)),
+        in_specs=[vm] * 5, out_specs=(vm,) * 5, scratch_shapes=scratch,
+        compiler_params=pltpu.CompilerParams(collective_id=cid, has_side_effects=True, vmem_limit_bytes=40 << 20),
+        name="reduce_all",
+    )(gw_qkv, gw_out, up_sum, down_sum, small)
 
 
 def pack_heads(block, b, c):
@@ -599,13 +763,11 @@
     qk_two, v_two, out_two, small = cube_one(flip_y, qk_one), cube_one(flip_x, v_one), cube_one(flip_x, out_one), cube_one(flip_y, small)
     qk_all, v_all, out_all, small = cube_one(flip_x, qk_two), cube_one(flip_y, v_two), cube_one(flip_y, out_two), cube_one(flip_x, small)
     wqk, wv, wo = arrange(spot, [(qk_all, True), (v_all, False), (out_all, False)])
-    wqk, wv, wo = wqk.reshape(width, 512), wv.reshape(width, 256), wo.reshape(256, width)
+    wqkv, wo = jnp.concatenate([wqk.reshape(width, 512), wv.reshape(width, 256)], 1), wo.reshape(256, width)
 
     up = w_up.reshape(32, 2, 2, 2, 2, 2, 128).transpose(2, 4, 0, 1, 3, 5, 6).reshape(2, 2, 32, 1024)
     up_block = sort_ranks(to_ranks(after(up, qkv_block), b, c), b, c)
     up_one, down_one = cube_start(after(up_block, qk_one)), cube_start(after(w_down, qk_one))
-    up_two, down_two = cube_one(flip_y, after(up_one, qk_all)), cube_one(flip_x, after(down_one, v_all))
-
     small = small.reshape(2, 2, 2, 2, 2, 16, 128).astype(f32)
     for axis, flag in enumerate((x, y, a, b, c)):
         small = swap_if(flag, small, axis)
@@ -619,20 +781,24 @@
 
     hidden = tokens[0].astype(f32)
     first = norm_rows(rows.astype(f32), gains[0], shifts[0]).astype(bf16)
-    qk = (dot_nn(first, wqk) + qk_shift).astype(bf16)
-    v = (dot_nn(first, wv) + v_shift).astype(bf16)
+    up_two, down_two = cube_one(flip_x, up_one), cube_one(flip_y, down_one)
+    first = after(first, up_one, down_one)
+    projected = (dot_nn(first, wqkv) + jnp.concatenate([qk_shift, v_shift])).astype(bf16)
+    qk, v = projected[:, :512], projected[:, 512:]
     qk = sort_ranks(qk.reshape(2, 2, 128, 4, 128), b, c).transpose(3, 0, 1, 2, 4).reshape(4, 2, 256, 128)
-    packed = exchange(jnp.concatenate([qk, pack_heads(v, b, c)], 2), True, 1).reshape(8, 384, 128)
-    attended = exchange(attend(valid[None], packed).reshape(2, 2, 2, 128, 128), False, 2)
+    packed = exchange(after(jnp.concatenate([qk, pack_heads(v, b, c)], 2), up_two, down_two), True, 1).reshape(8, 384, 128)
+    down_all = cube_one(flip_x, down_two)
+    attended = attend(valid[None], packed).reshape(2, 2, 2, 128, 128)
+    attended = exchange(after(attended, down_all), False, 2)
     attended = sort_ranks(unpack_heads(attended), b, c).reshape(512, 256)
 
-    up_all, down_all = cube_one(flip_x, up_two), cube_one(flip_y, after(down_two, attended))
+    up_all = cube_one(flip_y, after(up_two, attended))
     branch = scatter_rows(dot_nn(attended, wo)) + out_full
     second, pull_second = jax.vjp(norm_rows, branch, gains[1], shifts[1])
     middle = hidden + second
     third, pull_third = jax.vjp(norm_rows, middle, gains[2], shifts[2])
     third = gather_rows(third.astype(bf16))
-    wu, wd = arrange(spot, [(up_all, True), (down_all, False)])
+    wu, wd = arrange(spot, [(up_all, False), (down_all, True)])
     wu, wd = wu.reshape(width, 1024), wd.reshape(1024, width)
     up_pre = dot_nn(third, wu) + up_shift
     active, pull_gelu = jax.vjp(exact_gelu, up_pre)
@@ -647,49 +813,35 @@
     grad_down = grad_down.astype(bf16)
     down_rows = gather_rows(grad_down)
     gw_down = contract_rows(active, down_rows).astype(bf16).reshape(2, 2, 2, 128, width)
-    down_sum = fold(gw_down, flip_y, y, 1)
-    (grad_up,) = pull_gelu(dot_nt(down_rows, wd))
+    down_term = flip_y(pick(gw_down, 1 - y, 1, True))
+    (grad_up,) = pull_gelu(dot_nt(after(down_rows, gw_down), wd))
     grad_up = grad_up.astype(bf16)
     gw_up = contract_rows(third, grad_up).astype(bf16).reshape(2, 2, 2, 2, 2, 32, 1024)
-    up_sum = fold(gw_up, flip_x, x, 4)
-    part, gain3, shift3 = pull_third(scatter_rows(dot_nt(grad_up, wu)))
+    up_term = flip_x(pick(gw_up, 1 - x, 4, True))
+    part, gain3, shift3 = pull_third(scatter_rows(dot_nt(after(grad_up, gw_up), wu)))
     grad_middle = grad_out + part
     grad_branch, gain2, shift2 = pull_second(grad_middle)
     grad_branch = grad_branch.astype(bf16)
     branch_rows = gather_rows(grad_branch)
     grad_att = dot_nt(branch_rows, wo).astype(bf16)
-    grad_packed = exchange(pack_heads(grad_att, b, c), True, 3).reshape(8, 128, 128)
+    down_sum = add_low(pick(gw_down, y, 1, True), down_term)
+    grad_packed = exchange(after(pack_heads(grad_att, b, c), down_sum), True, 3).reshape(8, 128, 128)
+    up_sum = add_low(pick(gw_up, x, 4, True), after(up_term, grad_packed))
     back = attend_back(valid[None], packed, grad_packed)
 
-    up_sum = fold(after(up_sum, grad_packed), flip_y, y, 2)
-    down_sum = fold(after(down_sum, grad_packed), flip_x, x, 2)
+    up_sum = fold(up_sum, flip_y, y, 2)
+    down_sum = fold(down_sum, flip_x, x, 2)
+    back = after(back, up_sum)
     gw_out = contract_rows(attended, branch_rows).astype(bf16).reshape(2, 2, 2, 32, width)
     back = exchange(back.reshape(2, 2, 2, 384, 128), False, 4)
     grad_qk = back[:, :, :256].reshape(4, 2, 2, 128, 128).transpose(1, 2, 3, 0, 4).reshape(2, 2, 128, 512)
     grad_qk = sort_ranks(grad_qk, b, c).reshape(512, 512)
     grad_v = sort_ranks(unpack_heads(back[:, :, 256:]), b, c).reshape(512, 256)
-    gw_qk = contract_rows(first, grad_qk).astype(bf16).reshape(2, 2, 2, 2, 2, 32, 512)
-    gw_v = contract_rows(first, grad_v).astype(bf16).reshape(2, 2, 2, 2, 2, 32, 256)
+    grad_qkv = jnp.concatenate([grad_qk, grad_v], 1)
+    gw_qkv = contract_rows(first, grad_qkv).astype(bf16).reshape(2, 2, 2, 2, 2, 32, 768)
     _, pull_first = jax.vjp(norm_rows, hidden, gains[0], shifts[0])
-    part, gain1, shift1 = pull_first(scatter_rows(dot_nt(grad_qk, wqk) + dot_nt(grad_v, wv)))
+    part, gain1, shift1 = pull_first(scatter_rows(dot_nt(grad_qkv, wqkv)))
     input_grad = (grad_middle + part).astype(bf16)
-
-    out_sum = fold(fold(gw_out, flip_y, y, 1), flip_x, x, 2)
-    qk_sum = fold(fold(gw_qk, flip_x, x, 4), flip_y, y, 2)
-    v_sum = fold(fold(gw_v, flip_y, y, 2), flip_x, x, 4)
-    r_qk = fold_last(qk_sum, flip_a, a, 0).reshape(2, 2, 32, 512)
-    r_v = fold_last(v_sum, flip_a, a, 0).reshape(2, 2, 32, 256)
-    r_out = fold_last(out_sum, flip_a, a, 0).reshape(32, width)
-    r_up = fold_last(after(up_sum, back), flip_a, a, 0).reshape(2, 2, 32, 1024)
-    r_down = fold_last(after(down_sum, back), flip_a, a, 0).reshape(128, width)
-
-    def own_columns(block):
-        return sort_ranks(to_ranks(block, b, c), b, c)
-
-    r_qkv = own_columns(jnp.concatenate([r_qk, r_v], 3))
-    r_up = own_columns(r_up).reshape(2, 2, 32, 2, 2, 2, 128).transpose(2, 3, 0, 4, 1, 5, 6).reshape(32, 4096)
-    out_qk = r_qkv[..., :512].reshape(2, 2, 32, 2, 2, 2, HD).transpose(2, 5, 3, 0, 4, 1, 6).reshape(32, 2048)
-    out_v = r_qkv[..., 512:].reshape(2, 2, 32, 2, 2, HD).transpose(2, 3, 0, 4, 1, 5).reshape(32, 1024)
 
     def in_ranks(block, axes):
         for axis, flag in axes:
@@ -710,9 +862,10 @@
     sums_up = jnp.broadcast_to(jnp.sum(grad_up.astype(f32), 0).reshape(2, 1, 2, 1, 2, 1, 128), (2, 2, 2, 2, 2, 1, 128))
     sums_up = in_ranks(sums_up, ((1, b), (3, c)))
     terms = jnp.concatenate([vecs, sums_up, jnp.zeros((2, 2, 2, 2, 2, 4, 128), f32)], 5)
-    for flip_one, index, axis in ((flip_x, x, 4), (flip_y, y, 2), (flip_a, a, 0), (flip_b, b, 1), (flip_core, c, 3)):
-        terms = pick(terms, index, axis, True) + flip_one(pick(terms, 1 - index, axis, True))
-    small = terms.reshape(8, 128)
+    r_qkv, r_out, r_up, r_down, small = reduce_all(gw_qkv, gw_out, up_sum[:, :, 0, :, 0], down_sum[:, 0, 0], terms, 5)
+    r_up = r_up.reshape(2, 2, 32, 2, 2, 2, 128).transpose(2, 3, 0, 4, 1, 5, 6).reshape(32, 4096)
+    out_qk = r_qkv[..., :512].reshape(2, 2, 32, 2, 2, 2, HD).transpose(2, 5, 3, 0, 4, 1, 6).reshape(32, 2048)
+    out_v = r_qkv[..., 512:].reshape(2, 2, 32, 2, 2, HD).transpose(2, 3, 0, 4, 1, 5).reshape(32, 1024)
     vectors = small[:3].reshape(12, 32)
 
     return (

time: 419 us -> 408 us (0.974)
  Pallas kernels: 81 us -> 128 us
  waiting for transfers between devices: 131 us -> 94.8 us
  starting transfers between devices: 62.5 us -> 47.6 us
    pallas_call x0 -> x1, Pallas kernels: none -> 41 us  [reduce_all(): pl.pallas_call(reduce_kernel, out_shape=(S((2, 2) + q, f32), S((o[0], 102...]
    ppermute x12 -> x8, waiting for transfers between devices: 27.4 us -> 4.09 us  [flip_x(): return lax.ppermute(block, 'dp', [(0, 1), (1, 0)])]
    ppermute x65 -> x47, waiting for transfers between devices: 103 us -> 90.7 us  [flip(): return lax.ppermute(block, 'seq', [(s, s ^ bits) for s in range(16)])]
    ppermute x12 -> x8, starting transfers between devices: 17.5 us -> 9.18 us  [flip_x(): return lax.ppermute(block, 'dp', [(0, 1), (1, 0)])]
    ppermute x65 -> x47, starting transfers between devices: 45 us -> 38.4 us  [flip(): return lax.ppermute(block, 'seq', [(s, s ^ bits) for s in range(16)])]
    pallas_call x4, Pallas kernels: 58.1 us -> 64.1 us  [exchange(): pl.pallas_call(functools.partial(exchange_kernel, scatter), out_shape=jax...]
    unnamed x137 -> x161, local copies, waits for them, and re-layouts: 7.91 us -> 13.4 us
    concatenate x11, local copies, waits for them, and re-layouts: 8.62 us -> 3.82 us  [fast_body(): vecs = jnp.concatenate([head_sums(grad_qk), head_sums(grad_v), whole], 0)]
  transfers between devices with their start and end apart: 77 -> 55, of which waited for: 38 -> 26; matrix products, arithmetic and copies ran while one was open for 20% -> 16% of each run, Pallas kernels for 9% -> 19%
where the time goes in v2:
time: 408 us; the launch traced here: 400 us
  Pallas kernels  128 us (31%)
  waiting for transfers between devices  94.8 us (23%)
  local copies, waits for them, and re-layouts  56.6 us (14%)
  starting transfers between devices  47.6 us (12%)
  other arithmetic  40.8 us (10%)
  matrix products  27.5 us (7%)
  between operations  4.77 us (1%)
    ppermute x47, waiting for transfers between devices, flip(): return lax.ppermute(block, 'seq', [(s, s ^ bits) for s in range(16)])  90.7 us
    pallas_call x4, Pallas kernels, exchange(): pl.pallas_call(functools.partial(exchange_kernel, scatter), out_shape=jax...  64.1 us
    pallas_call x1, Pallas kernels, reduce_all(): pl.pallas_call(reduce_kernel, out_shape=(S((2, 2) + q, f32), S((o[0], 102...  41 us
    ppermute x47, starting transfers between devices, flip(): return lax.ppermute(block, 'seq', [(s, s ^ bits) for s in range(16)])  38.4 us
    unnamed x161, local copies, waits for them, and re-layouts  13.4 us
    pallas_call x1, Pallas kernels, attend_back(): pl.pallas_call(attend_back_kernel, out_shape=jax.ShapeDtypeStruct(packed....  11.6 us
    dot_general x4, matrix products, dot_nn(): return jnp.dot(a, b, preferred_element_type=jnp.float32)  11.3 us
    dot_general x4, matrix products, contract_rows(): lax.dot_general(left, right, (((0,), (0,)), ((), ())), preferred_element_...  9.38 us
  transfers between devices with their start and end apart: 55, of which 26 were waited for; matrix products, arithmetic and copies ran while one was open for 16% of the time, Pallas kernels for 19%

profile of v2, /device:TPU:0, one launch (start us, length us, event | category | flops | bytes accessed | tf_op | source)
XLA Modules:
  0.0 400.1 jit_solution(2181241617918080206)
XLA Ops:
  5.6 2.6 collective-permute-start.4
  8.4 2.9 collective-permute-start.23
  22.3 2.2 collective-permute-done.10
  36.3 2.1 collective-permute-done.20
  47.6 14.4 %collective-permute-done.17 = bf16[128,1024]{1,0:T(8,128)(2,1)S(1)} collective-permute-done((bf16[128,1024]{1,0:T(8,128)(2,1)S(1)}, bf16[128,1024]{1,0:T(8,128)(2,1)S(1)}, u32[]{:S(2)}, u32[]{:S(2)}) %collective-permute-start.17) | collective-permute-done | bytes 262176 | tf_op jit(solution)/shard_map/ppermute | solution.py:457
  64.9 2.6 collective-permute-done.16
  72.7 3.0 collective-permute-done.22
  78.5 3.8 collective-permute-done.19
  86.5 2.3 collective-permute-done.27
  95.3 2.2 pad_maximum_fusion.5
  97.5 21.4 %exchange.4 = bf16[2,2,2,384,128]{4,3,2,1,0:T(8,128)(2,1)} custom-call(bf16[4,2,384,128]{3,2,1,0:T(8,128)(2,1)} %pad_maximum_fusion.12.src), custom_call_target="tpu_custom_call" | custom-call | bytes 38400000 | tf_op jit(solution)/shard_map/exchange/pallas_call | solution.py:336
  120.1 8.0 %attend.1 = bf16[8,128,128]{2,1,0:T(8,128)(2,1)S(1)} custom-call(s32[1]{0:T(128)} %dynamic_slice.87.valid_ref, bf16[8,384,128]{2,1,0:T(8,128)(2,1)S(1)} %bitcast.263), custom_call_target="tpu_custom_call" | custom-call | tf_op jit(solution)/shard_map/attend/pallas_call | solution.py:432
  130.4 10.0 %exchange.5 = bf16[4,2,128,128]{3,2,1,0:T(8,128)(2,1)} custom-call(bf16[2,2,2,128,128]{4,3,2,1,0:T(8,128)(2,1)} %bitcast.269), custom_call_target="tpu_custom_call" | custom-call | bytes 12800000 | tf_op jit(solution)/shard_map/exchange/pallas_call | solution.py:336
  148.0 5.6 %collective-permute-done.31 = bf16[128,1024]{1,0:T(8,128)(2,1)} collective-permute-done((bf16[128,1024]{1,0:T(8,128)(2,1)S(1)}, bf16[128,1024]{1,0:T(8,128)(2,1)}, u32[]{:S(2)}, u32[]{:S(2)}) %collective-permute-start.31) | collective-permute-done | bytes 262176 | tf_op jit(solution)/shard_map/ppermute | solution.py:457
  157.4 6.2 %collective-permute-done.33 = bf16[128,1024]{1,0:T(8,128)(2,1)S(1)} collective-permute-done((bf16[128,1024]{1,0:T(8,128)(2,1)S(1)}, bf16[128,1024]{1,0:T(8,128)(2,1)S(1)}, u32[]{:S(2)}, u32[]{:S(2)}) %collective-permute-start.33) | collective-permute-done | bytes 262176 | tf_op jit(solution)/shard_map/ppermute | solution.py:457
  163.6 8.2 %collective-permute-done.35 = bf16[4,2,2,32,1024]{4,3,2,1,0:T(8,128)(2,1)S(1)} collective-permute-done((bf16[4,2,2,32,1024]{4,3,2,1,0:T(8,128)(2,1)}, bf16[4,2,2,32,1024]{4,3,2,1,0:T(8,128)(2,1)S(1)}, u32[]{:S(2)}, u32[]{:S(2)}) %collective-permute-start.35) | collective-permute-done | bytes 1048608 | tf_op jit(solution)/shard_map/ppermute | solution.py:457
  173.6 8.6 %multiply_convert_fusion = (bf16[512,1024]{1,0:T(8,128)(2,1)S(1)}, f32[512,1024]{1,0:T(8,128)}, f32[512,1024]{1,0:T(8,128)}) fusion(f32[1024]{0:T(1024)S(1)} %bitcast.350, bf16[1024,1024]{1,0:T(8,128)(2,1)S(1)} %bitcast.273, bf16[128,1024]{1,0:T(8,128)(2,1)S(1)} %collective-permute-done.34, bf16[128,1024]{1,0:T(8,128)(2,1)S(1)} %collective-permute-done.33, ...), kind=kOutput, calls=%fused_computation.16 | convolution fusion | flops 1112539136 | bytes 8392704 | tf_op jit(solution)/shard_map/dot_general | solution.py:351
  188.4 5.8 %collective-permute-done.38 = bf16[128,1024]{1,0:T(8,128)(2,1)} collective-permute-done((bf16[128,1024]{1,0:T(8,128)(2,1)S(1)}, bf16[128,1024]{1,0:T(8,128)(2,1)}, u32[]{:S(2)}, u32[]{:S(2)}) %collective-permute-start.38) | collective-permute-done | bytes 262176 | tf_op jit(solution)/shard_map/ppermute | solution.py:457
  199.1 5.8 %collective-permute-done.40 = bf16[128,1024]{1,0:T(8,128)(2,1)S(1)} collective-permute-done((bf16[128,1024]{1,0:T(8,128)(2,1)S(1)}, bf16[128,1024]{1,0:T(8,128)(2,1)S(1)}, u32[]{:S(2)}, u32[]{:S(2)}) %collective-permute-start.40) | collective-permute-done | bytes 262176 | tf_op jit(solution)/shard_map/ppermute | solution.py:457
  206.4 2.7 convolution_convert_fusion.1
  212.8 2.6 convolution_convert_fusion
  237.3 3.9 collective-permute-done.46
  241.2 10.1 %collective-permute-done.48 = bf16[2,1,2,128,1024]{4,3,0,2,1:T(8,128)(2,1)} collective-permute-done((bf16[2,1,2,128,1024]{4,3,0,2,1:T(8,128)(2,1)}, bf16[2,1,2,128,1024]{4,3,0,2,1:T(8,128)(2,1)}, u32[]{:S(2)}, u32[]{:S(2)}) %collective-permute-start.48) | collective-permute-done | bytes 1048608 | tf_op jit(solution)/shard_map/ppermute | solution.py:457
  251.2 2.6 add_convert_fusion.1
  259.3 10.8 %exchange.6 = bf16[2,2,2,128,128]{4,3,2,1,0:T(8,128)(2,1)} custom-call(bf16[4,2,128,128]{3,2,1,0:T(8,128)(2,1)} %copy.85.src), custom_call_target="tpu_custom_call" | custom-call | bytes 12800000 | tf_op jit(solution)/shard_map/exchange/pallas_call | solution.py:336
  276.3 11.6 %attend_back.1 = bf16[8,384,128]{2,1,0:T(8,128)(2,1)S(1)} custom-call(s32[1]{0:T(128)} %dynamic_slice.87.valid_ref, bf16[8,384,128]{2,1,0:T(8,128)(2,1)S(1)} %bitcast.264, bf16[8,128,128]{2,1,0:T(8,128)(2,1)S(1)} %bitcast.268), custom_call_target="tpu_custom_call" | custom-call | tf_op jit(solution)/shard_map/attend_back/pallas_call | solution.py:445
  289.8 21.9 %exchange.7 = bf16[4,2,384,128]{3,2,1,0:T(8,128)(2,1)} custom-call(bf16[2,2,2,384,128]{4,3,2,1,0:T(8,128)(2,1)} %bitcast.265), custom_call_target="tpu_custom_call" | custom-call | bytes 38400000 | tf_op jit(solution)/shard_map/exchange/pallas_call | solution.py:336
  320.0 2.1 fusion.12
  329.5 2.5 convolution_convert_fusion.2
  331.9 6.2 %collective-permute-done.53 = bf16[128,1024]{1,0:T(8,128)(2,1)S(1)} collective-permute-done((bf16[128,1024]{1,0:T(8,128)(2,1)S(1)}, bf16[128,1024]{1,0:T(8,128)(2,1)S(1)}, u32[]{:S(2)}, u32[]{:S(2)}) %collective-permute-start.53) | collective-permute-done | bytes 262176 | tf_op jit(solution)/shard_map/ppermute | solution.py:457
  344.5 41.0 %reduce_all.1 = (f32[2,2,32,768]{3,2,1,0:T(8,128)S(1)}, f32[32,1024]{1,0:T(8,128)S(1)}, f32[2,2,32,1024]{3,2,1,0:T(8,128)S(1)}, f32[128,1024]{1,0:T(8,128)S(1)}, f32[8,128]{1,0:T(8,128)S(1)}) custom-call(bf16[2,2,2,2,2,32,768]{6,5,4,3,2,1,0:T(8,128)(2,1)S(1)} %bitcast.267, bf16[2,2,2,32,1024]{4,3,2,1,0:T(8,128)(2,1)S(1)} %bitcast.270, ...), custom_call_target="tpu_custom_call" | custom-call | tf_op jit(solution)/shard_map/reduce_all/pallas_call | solution.py:724
  390.1 2.2 fusion.52
  (477 shorter events, 157.5 us)
Async XLA Ops:
  5.1 8.9 %collective-permute-start.3 = (bf16[16,128]{1,0:T(8,128)(2,1)S(1)}, bf16[16,128]{1,0:T(8,128)(2,1)S(1)}, u32[]{:S(2)}, u32[]{:S(2)}) collective-permute-start(bf16[16,128]{1,0:T(8,128)(2,1)S(1)} %get-tuple-element.143), channel_id=1, source_target_pairs={{0,2},{2,0},{4,6},{6,4},{8,10},{10,8},{12,14},{14,12},{16,18},{18,... | collective-permute-start | bytes 12296 | tf_op jit(solution)/shard_map/ppermute | solution.py:457
  5.6 8.0 %collective-permute-start.4 = (bf16[16,128]{1,0:T(8,128)(2,1)S(1)}, bf16[16,128]{1,0:T(8,128)(2,1)S(1)}, u32[]{:S(2)}, u32[]{:S(2)}) collective-permute-start(bf16[16,128]{1,0:T(8,128)(2,1)S(1)} %get-tuple-element.143), channel_id=1, source_target_pairs={{0,8},{2,10},{4,12},{6,14},{8,0},{10,2},{12,4},{14,6},{16,24},{18,... | collective-permute-start | bytes 12296 | tf_op jit(solution)/shard_map/ppermute | solution.py:457
  8.3 56.1 %collective-permute-start.1 = (bf16[128,1024]{1,0:T(8,128)(2,1)}, bf16[128,1024]{1,0:T(8,128)(2,1)S(1)}, u32[]{:S(2)}, u32[]{:S(2)}) collective-permute-start(bf16[128,1024]{1,0:T(8,128)(2,1)} %bitcast.281), channel_id=1, source_target_pairs={{0,8},{2,10},{4,12},{6,14},{8,0},{10,2},{12,4},{14,6},{16,24},{18,... | collective-permute-start | bytes 786440 | tf_op jit(solution)/shard_map/ppermute | solution.py:457
  8.3 69.0 %collective-permute-start = (bf16[128,1024]{1,0:T(8,128)(2,1)}, bf16[128,1024]{1,0:T(8,128)(2,1)S(1)}, u32[]{:S(2)}, u32[]{:S(2)}) collective-permute-start(bf16[128,1024]{1,0:T(8,128)(2,1)} %bitcast.282), channel_id=1, source_target_pairs={{0,2},{2,0},{4,6},{6,4},{8,10},{10,8},{12,14},{14,12},{16,18},{18,... | collective-permute-start | bytes 786440 | tf_op jit(solution)/shard_map/ppermute | solution.py:457
  8.4 21.8 %collective-permute-start.23 = (bf16[32,1024]{1,0:T(8,128)(2,1)}, bf16[32,1024]{1,0:T(8,128)(2,1)S(1)}, u32[]{:S(2)}, u32[]{:S(2)}) collective-permute-start(bf16[32,1024]{1,0:T(8,128)(2,1)} %param.20), channel_id=1, source_target_pairs={{0,16},{2,18},{4,20},{6,22},{8,24},{10,26},{12,28},{14,30},{16,0},... | collective-permute-start | bytes 196616 | tf_op jit(solution)/shard_map/ppermute | solution.py:457
  14.0 8.3 %collective-permute-start.11 = (bf16[32,768]{1,0:T(8,128)(2,1)S(1)}, bf16[32,768]{1,0:T(8,128)(2,1)S(1)}, u32[]{:S(2)}, u32[]{:S(2)}) collective-permute-start(bf16[32,768]{1,0:T(8,128)(2,1)S(1)} %get-tuple-element.132), channel_id=1, source_target_pairs={{0,10},{2,8},{4,14},{6,12},{8,2},{10,0},{12,6},{14,4},{16,26},{18,... | collective-permute-start | bytes 147464 | tf_op jit(solution)/shard_map/ppermute | solution.py:457
  30.4 8.0 %collective-permute-start.20 = (bf16[2,2,32,256]{3,2,1,0:T(8,128)(2,1)S(1)}, bf16[2,2,32,256]{3,2,1,0:T(8,128)(2,1)S(1)}, u32[]{:S(2)}, u32[]{:S(2)}) collective-permute-start(bf16[2,2,32,256]{3,2,1,0:T(8,128)(2,1)S(1)} %get-tuple-element.128), channel_id=1, source_target_pairs={{0,16},{2,18},{4,20},{6,22},{8,24},{10,26},{12,28},{14,30},{16,0},... | collective-permute-start | bytes 196616 | tf_op jit(solution)/shard_map/ppermute | solution.py:457
  32.6 10.2 %collective-permute-start.15 = (bf16[2,2,32,512]{3,2,1,0:T(8,128)(2,1)S(1)}, bf16[2,2,32,512]{3,2,1,0:T(8,128)(2,1)S(1)}, u32[]{:S(2)}, u32[]{:S(2)}) collective-permute-start(bf16[2,2,32,512]{3,2,1,0:T(8,128)(2,1)S(1)} %get-tuple-element.130), channel_id=1, source_target_pairs={{0,16},{2,18},{4,20},{6,22},{8,24},{10,26},{12,28},{14,30},{16,0},... | collective-permute-start | bytes 393224 | tf_op jit(solution)/shard_map/ppermute | solution.py:457
  42.9 19.1 %collective-permute-start.17 = (bf16[128,1024]{1,0:T(8,128)(2,1)S(1)}, bf16[128,1024]{1,0:T(8,128)(2,1)S(1)}, u32[]{:S(2)}, u32[]{:S(2)}) collective-permute-start(bf16[128,1024]{1,0:T(8,128)(2,1)S(1)} %copy-done.29), channel_id=1, source_target_pairs={{0,16},{2,18},{4,20},{6,22},{8,24},{10,26},{12,28},{14,30},{16,0},... | collective-permute-start | bytes 786440 | tf_op jit(solution)/shard_map/ppermute | solution.py:457
  44.8 20.0 %collective-permute-start.18 = (bf16[2,2,2,32,512]{4,3,2,1,0:T(8,128)(2,1)S(1)}, bf16[2,2,2,32,512]{4,3,2,1,0:T(8,128)(2,1)S(1)}, u32[]{:S(2)}, u32[]{:S(2)}) collective-permute-start(bf16[2,2,2,32,512]{4,3,2,1,0:T(8,128)(2,1)S(1)} %pad_maximum_fusion.23), channel_id=1, source_target_pairs={{0,4},{2,6},{4,0},{6,2},{8,12},{10,14},{12,8},{14,10},{16,20},{18,... | collective-permute-start | bytes 786440 | tf_op jit(solution)/shard_map/ppermute | solution.py:457
  46.4 21.1 %collective-permute-start.16 = (bf16[2,2,32,1024]{3,2,1,0:T(8,128)(2,1)S(1)}, bf16[2,2,32,1024]{3,2,1,0:T(8,128)(2,1)S(1)}, u32[]{:S(2)}, u32[]{:S(2)}) collective-permute-start(bf16[2,2,32,1024]{3,2,1,0:T(8,128)(2,1)S(1)} %reverse_select_fusion.8), channel_id=1, source_target_pairs={{0,16},{2,18},{4,20},{6,22},{8,24},{10,26},{12,28},{14,30},{16,0},... | collective-permute-start | bytes 786440 | tf_op jit(solution)/shard_map/ppermute | solution.py:457
  61.9 9.2 %collective-permute-start.25 = (bf16[4,32,1024]{2,1,0:T(8,128)(2,1)S(1)}, bf16[4,32,1024]{2,1,0:T(8,128)(2,1)S(1)}, u32[]{:S(2)}, u32[]{:S(2)}) collective-permute-start(bf16[4,32,1024]{2,1,0:T(8,128)(2,1)S(1)} %pad_maximum_fusion.25), channel_id=1, source_target_pairs={{0,4},{2,6},{4,0},{6,2},{8,12},{10,14},{12,8},{14,10},{16,20},{18,... | collective-permute-start | bytes 786440 | tf_op jit(solution)/shard_map/ppermute | solution.py:457
  64.3 11.3 %collective-permute-start.22 = (bf16[4,2,2,32,256]{4,3,2,1,0:T(8,128)(2,1)S(1)}, bf16[4,2,2,32,256]{4,3,2,1,0:T(8,128)(2,1)S(1)}, u32[]{:S(2)}, u32[]{:S(2)}) collective-permute-start(bf16[4,2,2,32,256]{4,3,2,1,0:T(8,128)(2,1)S(1)} %pad_maximum_fusion.24), channel_id=1, source_target_pairs={{0,4},{2,6},{4,0},{6,2},{8,12},{10,14},{12,8},{14,10},{16,20},{18,... | collective-permute-start | bytes 786440 | tf_op jit(solution)/shard_map/ppermute | solution.py:457
  64.8 12.5 %collective-permute-start.2 = (bf16[128,1024]{1,0:T(8,128)(2,1)S(1)}, bf16[128,1024]{1,0:T(8,128)(2,1)S(1)}, u32[]{:S(2)}, u32[]{:S(2)}) collective-permute-start(bf16[128,1024]{1,0:T(8,128)(2,1)S(1)} %collective-permute-done.1), channel_id=1, source_target_pairs={{0,2},{2,0},{4,6},{6,4},{8,10},{10,8},{12,14},{14,12},{16,18},{18,... | collective-permute-start | bytes 786440 | tf_op jit(solution)/shard_map/ppermute | solution.py:457
  67.5 14.8 %collective-permute-start.19 = (bf16[4,2,2,32,512]{4,3,2,1,0:T(8,128)(2,1)S(1)}, bf16[4,2,2,32,512]{4,3,2,1,0:T(8,128)(2,1)S(1)}, u32[]{:S(2)}, u32[]{:S(2)}) collective-permute-start(bf16[4,2,2,32,512]{4,3,2,1,0:T(8,128)(2,1)S(1)} %pad_maximum_fusion.16), channel_id=1, source_target_pairs={{0,1},{1,0},{2,3},{3,2},{4,5},{5,4},{6,7},{7,6},{8,9},{9,8},{10,11... | collective-permute-start | bytes 1572872 | tf_op jit(solution)/shard_map/ppermute | solution.py:464
  71.1 24.2 %collective-permute-start.26 = (bf16[2,2,2,32,1024]{4,3,2,1,0:T(8,128)(2,1)}, bf16[2,2,2,32,1024]{4,3,2,1,0:T(8,128)(2,1)}, u32[]{:S(2)}, u32[]{:S(2)}) collective-permute-start(bf16[2,2,2,32,1024]{4,3,2,1,0:T(8,128)(2,1)} %pad_maximum_fusion.14), channel_id=1, source_target_pairs={{0,1},{1,0},{2,3},{3,2},{4,5},{5,4},{6,7},{7,6},{8,9},{9,8},{10,11... | collective-permute-start | bytes 1572872 | tf_op jit(solution)/shard_map/ppermute | solution.py:464
  75.7 13.1 %collective-permute-start.27 = (bf16[2,128,1024]{2,1,0:T(8,128)(2,1)}, bf16[2,128,1024]{2,1,0:T(8,128)(2,1)S(1)}, u32[]{:S(2)}, u32[]{:S(2)}) collective-permute-start(bf16[2,128,1024]{2,1,0:T(8,128)(2,1)} %pad_maximum_fusion.15), channel_id=1, source_target_pairs={{0,4},{2,6},{4,0},{6,2},{8,12},{10,14},{12,8},{14,10},{16,20},{18,... | collective-permute-start | bytes 1572872 | tf_op jit(solution)/shard_map/ppermute | solution.py:457
  90.0 38.9 %collective-permute-start.28 = (bf16[4,128,1024]{2,1,0:T(8,128)(2,1)}, bf16[4,128,1024]{2,1,0:T(8,128)(2,1)}, u32[]{:S(2)}, u32[]{:S(2)}) collective-permute-start(bf16[4,128,1024]{2,1,0:T(8,128)(2,1)} %pad_maximum_fusion.6), channel_id=1, source_target_pairs={{0,1},{1,0},{2,3},{3,2},{4,5},{5,4},{6,7},{7,6},{8,9},{9,8},{10,11... | collective-permute-start | bytes 3145736 | tf_op jit(solution)/shard_map/ppermute | solution.py:464
  145.1 8.5 %collective-permute-start.31 = (bf16[128,1024]{1,0:T(8,128)(2,1)S(1)}, bf16[128,1024]{1,0:T(8,128)(2,1)}, u32[]{:S(2)}, u32[]{:S(2)}) collective-permute-start(bf16[128,1024]{1,0:T(8,128)(2,1)S(1)} %fusion.36), channel_id=1, source_target_pairs={{0,8},{2,10},{4,12},{6,14},{8,0},{10,2},{12,4},{14,6},{16,24},{18,... | collective-permute-start | bytes 786440 | tf_op jit(solution)/shard_map/ppermute | solution.py:457
  146.4 25.4 %collective-permute-start.35 = (bf16[4,2,2,32,1024]{4,3,2,1,0:T(8,128)(2,1)}, bf16[4,2,2,32,1024]{4,3,2,1,0:T(8,128)(2,1)S(1)}, u32[]{:S(2)}, u32[]{:S(2)}) collective-permute-start(bf16[4,2,2,32,1024]{4,3,2,1,0:T(8,128)(2,1)} %pad_maximum_fusion.5), channel_id=1, source_target_pairs={{0,4},{2,6},{4,0},{6,2},{8,12},{10,14},{12,8},{14,10},{16,20},{18,... | collective-permute-start | bytes 3145736 | tf_op jit(solution)/shard_map/ppermute | solution.py:457
  157.3 16.3 %collective-permute-start.32 = (bf16[128,1024]{1,0:T(8,128)(2,1)S(1)}, bf16[128,1024]{1,0:T(8,128)(2,1)S(1)}, u32[]{:S(2)}, u32[]{:S(2)}) collective-permute-start(bf16[128,1024]{1,0:T(8,128)(2,1)S(1)} %add_convert_fusion.10), channel_id=1, source_target_pairs={{0,2},{2,0},{4,6},{6,4},{8,10},{10,8},{12,14},{14,12},{16,18},{18,... | collective-permute-start | bytes 786440 | tf_op jit(solution)/shard_map/ppermute | solution.py:457
  163.6 10.0 %collective-permute-start.34 = (bf16[128,1024]{1,0:T(8,128)(2,1)S(1)}, bf16[128,1024]{1,0:T(8,128)(2,1)S(1)}, u32[]{:S(2)}, u32[]{:S(2)}) collective-permute-start(bf16[128,1024]{1,0:T(8,128)(2,1)S(1)} %collective-permute-done.33), channel_id=1, source_target_pairs={{0,2},{2,0},{4,6},{6,4},{8,10},{10,8},{12,14},{14,12},{16,18},{18,... | collective-permute-start | bytes 786440 | tf_op jit(solution)/shard_map/ppermute | solution.py:457
  185.7 8.5 %collective-permute-start.38 = (bf16[128,1024]{1,0:T(8,128)(2,1)S(1)}, bf16[128,1024]{1,0:T(8,128)(2,1)}, u32[]{:S(2)}, u32[]{:S(2)}) collective-permute-start(bf16[128,1024]{1,0:T(8,128)(2,1)S(1)} %fusion.31), channel_id=1, source_target_pairs={{0,8},{2,10},{4,12},{6,14},{8,0},{10,2},{12,4},{14,6},{16,24},{18,... | collective-permute-start | bytes 786440 | tf_op jit(solution)/shard_map/ppermute | solution.py:457
  218.6 8.9 %collective-permute-start.42 = (f32[128,1024]{1,0:T(8,128)}, f32[128,1024]{1,0:T(8,128)S(1)}, u32[]{:S(2)}, u32[]{:S(2)}) collective-permute-start(f32[128,1024]{1,0:T(8,128)} %get-tuple-element.115), channel_id=1, source_target_pairs={{0,2},{2,0},{4,6},{6,4},{8,10},{10,8},{12,14},{14,12},{16,18},{18,... | collective-permute-start | bytes 1572872 | tf_op jit(solution)/shard_map/ppermute | solution.py:457
  221.2 8.4 %collective-permute-start.44 = (bf16[128,1024]{1,0:T(8,128)(2,1)S(1)}, bf16[128,1024]{1,0:T(8,128)(2,1)S(1)}, u32[]{:S(2)}, u32[]{:S(2)}) collective-permute-start(bf16[128,1024]{1,0:T(8,128)(2,1)S(1)} %fusion.27), channel_id=1, source_target_pairs={{0,8},{2,10},{4,12},{6,14},{8,0},{10,2},{12,4},{14,6},{16,24},{18,... | collective-permute-start | bytes 786440 | tf_op jit(solution)/shard_map/ppermute | solution.py:457
  226.0 25.2 %collective-permute-start.48 = (bf16[2,1,2,128,1024]{4,3,0,2,1:T(8,128)(2,1)}, bf16[2,1,2,128,1024]{4,3,0,2,1:T(8,128)(2,1)}, u32[]{:S(2)}, u32[]{:S(2)}) collective-permute-start(bf16[2,1,2,128,1024]{4,3,0,2,1:T(8,128)(2,1)} %copy.101), channel_id=1, source_target_pairs={{0,4},{2,6},{4,0},{6,2},{8,12},{10,14},{12,8},{14,10},{16,20},{18,... | collective-permute-start | bytes 3145736 | tf_op jit(solution)/shard_map/ppermute | solution.py:457
  236.4 33.7 %collective-permute-start.49 = (bf16[2,2,2,2,1,32,1024]{6,5,3,1,0,4,2:T(8,128)(2,1)}, bf16[2,2,2,2,1,32,1024]{6,5,3,1,0,4,2:T(8,128)(2,1)}, u32[]{:S(2)}, u32[]{:S(2)}) collective-permute-start(bf16[2,2,2,2,1,32,1024]{6,5,3,1,0,4,2:T(8,128)(2,1)} %copy.103), channel_id=1, source_target_pairs={{0,1},{1,0},{2,3},{3,2},{4,5},{5,4},{6,7},{7,6},{8,9},{9,8},{10,11... | collective-permute-start | bytes 3145736 | tf_op jit(solution)/shard_map/ppermute | solution.py:464
  237.2 16.6 %collective-permute-start.45 = (bf16[128,1024]{1,0:T(8,128)(2,1)}, bf16[128,1024]{1,0:T(8,128)(2,1)S(1)}, u32[]{:S(2)}, u32[]{:S(2)}) collective-permute-start(bf16[128,1024]{1,0:T(8,128)(2,1)} %get-tuple-element.85), channel_id=1, source_target_pairs={{0,2},{2,0},{4,6},{6,4},{8,10},{10,8},{12,14},{14,12},{16,18},{18,... | collective-permute-start | bytes 786440 | tf_op jit(solution)/shard_map/ppermute | solution.py:457
  241.1 12.7 %collective-permute-start.47 = (bf16[128,1024]{1,0:T(8,128)(2,1)S(1)}, bf16[128,1024]{1,0:T(8,128)(2,1)S(1)}, u32[]{:S(2)}, u32[]{:S(2)}) collective-permute-start(bf16[128,1024]{1,0:T(8,128)(2,1)S(1)} %collective-permute-done.46), channel_id=1, source_target_pairs={{0,2},{2,0},{4,6},{6,4},{8,10},{10,8},{12,14},{14,12},{16,18},{18,... | collective-permute-start | bytes 786440 | tf_op jit(solution)/shard_map/ppermute | solution.py:457
  271.9 17.7 %collective-permute-start.50 = (bf16[2,2,1,2,1,32,1024]{6,5,3,1,0,4,2:T(8,128)(2,1)S(1)}, bf16[2,2,1,2,1,32,1024]{6,5,3,1,0,4,2:T(8,128)(2,1)S(1)}, u32[]{:S(2)}, u32[]{:S(2)}) collective-permute-start(bf16[2,2,1,2,1,32,1024]{6,5,3,1,0,4,2:T(8,128)(2,1)S(1)} %constant_dynamic-slice_fusion.2), channel_id=1, source_target_pairs={{0,4},{2,6},{4,0},{6,2},{8,12},{10,14},{12,8},{14,10},{16,20},{18,... | collective-permute-start | bytes 1572872 | tf_op jit(solution)/shard_map/ppermute | solution.py:457
  275.8 47.5 %collective-permute-start.54 = (bf16[2,1,1,128,1024]{4,3,0,2,1:T(8,128)(2,1)}, bf16[2,1,1,128,1024]{4,3,0,2,1:T(8,128)(2,1)}, u32[]{:S(2)}, u32[]{:S(2)}) collective-permute-start(bf16[2,1,1,128,1024]{4,3,0,2,1:T(8,128)(2,1)} %constant_dynamic-slice_fusion.1), channel_id=1, source_target_pairs={{0,1},{1,0},{2,3},{3,2},{4,5},{5,4},{6,7},{7,6},{8,9},{9,8},{10,11... | collective-permute-start | bytes 1572872 | tf_op jit(solution)/shard_map/ppermute | solution.py:464
  329.4 8.8 %collective-permute-start.53 = (bf16[128,1024]{1,0:T(8,128)(2,1)S(1)}, bf16[128,1024]{1,0:T(8,128)(2,1)S(1)}, u32[]{:S(2)}, u32[]{:S(2)}) collective-permute-start(bf16[128,1024]{1,0:T(8,128)(2,1)S(1)} %fusion.23), channel_id=1, source_target_pairs={{0,8},{2,10},{4,12},{6,14},{8,0},{10,2},{12,4},{14,6},{16,24},{18,... | collective-permute-start | bytes 786440 | tf_op jit(solution)/shard_map/ppermute | solution.py:457
  (102 other events, 714.5 us)

commit v3 on v2

--- a/solution.py
+++ b/solution.py
@@ -561,8 +561,8 @@
     return add_low(pick(terms, index, axis, True), flip_one(pick(terms, 1 - index, axis, True)))
 
 
-def reduce_kernel(q_ref, o_ref, u_ref, d_ref, s_ref, rq, ro, ru, rd, rs,
-                  r1q, t2q, r2q, t3q, r3q, fq, gq, r1o, t2o, r2o, t3o, r3o, r3u, fu, gu, r3d,
+def reduce_kernel(q_ref, o_ref, u_ref, d_ref, s_ref, out_q, ro, out_u, rd, rs,
+                  rq, ru, r1q, t2q, r2q, t3q, r3q, fq, gq, r1o, t2o, r2o, t3o, r3o, r3u, fu, gu, r3d,
                   sx, s1, sy, s2, sa, s3, sb, s4, sc, send_sem, recv_sem):
     a, b, y, c, x = place()
     f32, bf16 = jnp.float32, jnp.bfloat16
@@ -700,6 +700,17 @@
         pb, pc = ranks[k]
         qr[k - 1].wait_recv()
         rq[pb, pc] = gq[k - 1].astype(f32)
+    for pb in range(2):
+        for j in range(4):
+            zero, one = rq[pb, 0], rq[pb, 1]
+            h = head_of(j // 2, pb, j % 2, 0) * HD
+            q, k = slice(j * 128, j * 128 + HD), slice(j * 128 + HD, j * 128 + 128)
+            v = slice(512 + j * HD, 512 + j * HD + HD)
+            for t, cols in enumerate((q, k, v)):
+                out_q[:, t * 1024 + h:t * 1024 + h + 128] = jnp.concatenate([zero[:, cols], one[:, cols]], 1)
+            for pc in range(2):
+                col = head_of(j // 2, pb, j % 2, pc) * 256
+                out_u[:, col:col + 256] = ru[pb, pc, :, j * 256:j * 256 + 256]
     vc.wait_recv()
     rs[...] = s4[c] + sc[...]
     for copy in made:
@@ -714,6 +725,7 @@
     q, o = gw_qkv.shape[5:], (gw_out.shape[3], 512)
     u, d, s = up_sum.shape[1:], down_sum.shape[1:], small.shape[5:]
     scratch = [
+        V((2, 2) + q, f32), V(u, f32),
         V((2, 2, 2, 2) + q, bf16), V((2, 2, 2) + q, bf16), V((2, 2, 2) + q, bf16), V((2, 2) + q, bf16), V((2, 2) + q, bf16),
         V((2, 2) + q, bf16), V((3,) + q, bf16),
         V((2, 2, 2) + o, bf16), V((2, 2) + o, bf16), V((2, 2) + o, bf16), V((2,) + o, bf16), V((2,) + o, bf16),
@@ -723,11 +735,173 @@
         pltpu.SemaphoreType.DMA((33,)), pltpu.SemaphoreType.DMA((33,))]
     return pl.pallas_call(
         reduce_kernel,
-        out_shape=(S((2, 2) + q, f32), S((o[0], 1024), f32), S(u, f32), S(d, f32), S(s, f32)),
+        out_shape=(S((q[0], 4 * q[1]), f32), S((o[0], 1024), f32), S((u[2], 4 * u[3]), f32), S(d, f32), S(s, f32)),
         in_specs=[vm] * 5, out_specs=(vm,) * 5, scratch_shapes=scratch,
         compiler_params=pltpu.CompilerParams(collective_id=cid, has_side_effects=True, vmem_limit_bytes=40 << 20),
         name="reduce_all",
     )(gw_qkv, gw_out, up_sum, down_sum, small)
+
+
+def qk_columns(head):
+    return slice(head * HD, head * HD + HD), slice(1024 + head * HD, 1024 + head * HD + HD), slice(2048 + head * HD, 2048 + head * HD + HD)
+
+
+def head_of(a, b, y, c):
+    return a * 8 + b * 4 + y * 2 + c
+
+
+def start_kernel(q_in, u_in, o_in, t_in, v_in, wq, wo, up, rows, vec, q_src, u_src, send_sem, recv_sem, own_sem):
+    a, b, y, c, x = place()
+    barrier = pltpu.get_barrier_semaphore()
+
+    def at(pa, pb, py, pc, px):
+        return (pa * 8 + pb * 4 + py * 2 + pc, px)
+
+    to_x, to_y, to_a = at(a, b, y, c, 1 - x), at(a, b, 1 - y, c, x), at(1 - a, b, y, c, x)
+    ranks = [(lax.rem(b + k // 2, 2), lax.rem(c + k % 2, 2)) for k in range(4)]
+    to_rank = [at(a, pb, y, pc, x) for pb, pc in ranks]
+    for dev in [to_x, to_y, to_a] + to_rank[1:]:
+        pl.semaphore_signal(barrier, inc=1, device_id=dev, device_id_type=MESH)
+
+    for pb in range(2):
+        for pc in range(2):
+            for j in range(4):
+                q, k, v = qk_columns(head_of(j // 2, pb, j % 2, pc))
+                q_src[pb, pc, :, j * 128:j * 128 + 128] = jnp.concatenate([q_in[:, q], q_in[:, k]], 1)
+            for j in range(2):
+                v0 = qk_columns(head_of(j, pb, 0, pc))[2]
+                v1 = qk_columns(head_of(j, pb, 1, pc))[2]
+                q_src[pb, pc, :, 512 + j * 128:640 + j * 128] = jnp.concatenate([q_in[:, v0], q_in[:, v1]], 1)
+            for j in range(4):
+                col = (head_of(j // 2, pb, j % 2, pc)) * 256
+                u_src[pb, pc, :, j * 256:j * 256 + 256] = u_in[:, col:col + 256]
+    own = [pltpu.make_async_copy(src, dst, own_sem.at[k]) for k, (src, dst) in enumerate((
+        (q_src.at[b, c], wq.at[a, b, y, c, x]), (u_src.at[b, c], up.at[0, b, c]), (o_in, wo.at[a, y, x]),
+        (t_in, rows.at[0]), (v_in, vec.at[a, b, y, c, x])))]
+    for copy in own:
+        copy.start()
+    pl.semaphore_wait(barrier, 6)
+
+    made = []
+
+    def remote(src, dst, dev):
+        k = len(made)
+        made.append(pltpu.make_async_remote_copy(
+            src_ref=src, dst_ref=dst, send_sem=send_sem.at[k], recv_sem=recv_sem.at[k],
+            device_id=dev, device_id_type=MESH))
+        return made[-1]
+
+    places = [a, 1 - a]
+    halves = [slice(0, 512), slice(512, 1024)]
+    lateral = [(to_y, to_x), (to_x, to_y)]
+
+    def same(ref, dev):
+        return remote(ref, ref, dev)
+
+    q_rank = [remote(q_src.at[ranks[k][0], ranks[k][1]], wq.at[a, b, y, c, x], to_rank[k]) for k in range(1, 4)]
+    u_rank = [remote(u_src.at[ranks[k][0], ranks[k][1]], up.at[0, b, c], to_rank[k]) for k in range(1, 4)]
+    v_rank = [remote(v_in, vec.at[a, b, y, c, x], to_rank[k]) for k in range(1, 4)]
+    t_core, t_near = remote(t_in, rows.at[1], to_rank[1]), remote(t_in, rows.at[2], to_rank[2])
+    t_far = remote(rows.at[2], rows.at[3], to_rank[1])
+    u_cube = remote(up.at[0], up.at[1], to_a)
+    v_cube = [same(vec.at[a, :, y, :, x], to_a), same(vec.at[:, :, y, :, x], to_y), same(vec.at[:, :, :, :, x], to_x)]
+    q_cube = [same(wq.at[a, s, y, :, x], to_a) for s in range(2)]
+    o_cube = [remote(o_in.at[:, halves[s]], wo.at[a, y, x, :, halves[s]], to_a) for s in range(2)]
+    q_side, o_side = {}, {}
+    for i in range(2):
+        for s in range(2):
+            one, two = lateral[s]
+            oy, ox = (1 - y, x) if s == 0 else (y, 1 - x)
+            p = places[i]
+            mine, theirs = wq.at[p, s, y, :, x], wq.at[p, s, oy, :, ox]
+            q_side[s, i] = (same(mine, one), same(mine, two), same(theirs, two))
+            mine, theirs = wo.at[p, y, x, :, halves[s]], wo.at[p, oy, ox, :, halves[s]]
+            first = o_in.at[:, halves[s]] if i == 0 else mine
+            o_side[s, i] = (remote(first, mine, one), remote(first, mine, two), same(theirs, two))
+
+    for k in (2, 1, 0):
+        q_rank[k].start()
+        v_rank[k].start()
+    for s in range(2):
+        o_cube[s].start()
+        o_side[s, 0][0].start()
+        o_side[s, 0][1].start()
+    t_near.start()
+    t_core.start()
+    own[0].wait()
+    for copy in q_rank:
+        copy.wait_recv()
+    for s in range(2):
+        q_cube[s].start()
+        q_side[s, 0][0].start()
+        q_side[s, 0][1].start()
+    own[4].wait()
+    for copy in v_rank:
+        copy.wait_recv()
+    v_cube[0].start()
+    for k in (2, 1, 0):
+        u_rank[k].start()
+    for s in range(2):
+        o_side[s, 0][0].wait_recv()
+        o_side[s, 0][2].start()
+    for s in range(2):
+        o_cube[s].wait_recv()
+        o_side[s, 1][0].start()
+        o_side[s, 1][1].start()
+    t_near.wait_recv()
+    t_far.start()
+    for s in range(2):
+        q_side[s, 0][0].wait_recv()
+        q_side[s, 0][2].start()
+    for s in range(2):
+        q_cube[s].wait_recv()
+        q_side[s, 1][0].start()
+        q_side[s, 1][1].start()
+    v_cube[0].wait_recv()
+    v_cube[1].start()
+    own[1].wait()
+    for copy in u_rank:
+        copy.wait_recv()
+    u_cube.start()
+    for s in range(2):
+        o_side[s, 1][0].wait_recv()
+        o_side[s, 1][2].start()
+    v_cube[1].wait_recv()
+    v_cube[2].start()
+    for s in range(2):
+        q_side[s, 1][0].wait_recv()
+        q_side[s, 1][2].start()
+    v_cube[2].wait_recv()
+    t_core.wait_recv()
+    t_far.wait_recv()
+    for i in range(2):
+        for s in range(2):
+            for k in (1, 2):
+                q_side[s, i][k].wait_recv()
+                o_side[s, i][k].wait_recv()
+    u_cube.wait_recv()
+    own[2].wait()
+    own[3].wait()
+    for copy in made:
+        copy.wait_send()
+
+
+def start_gather(w_qkv, w_up, w_out, tokens, vectors, cid):
+    bf16 = jnp.bfloat16
+    S = lambda *shape: jax.ShapeDtypeStruct(shape, bf16)
+    vm, anywhere = pl.BlockSpec(memory_space=pltpu.VMEM), pl.BlockSpec(memory_space=pl.ANY)
+    return pl.pallas_call(
+        start_kernel,
+        out_shape=(S(2, 2, 2, 2, 2, 32, 768), S(2, 2, 2, 32, 1024), S(2, 2, 2, 32, 1024), S(4, 128, 1024),
+                   S(2, 2, 2, 2, 2, 16, 128)),
+        in_specs=[vm] * 5, out_specs=(anywhere,) * 5,
+        scratch_shapes=[
+            pltpu.VMEM((2, 2, 32, 768), bf16), pltpu.VMEM((2, 2, 32, 1024), bf16),
+            pltpu.SemaphoreType.DMA((48,)), pltpu.SemaphoreType.DMA((48,)), pltpu.SemaphoreType.DMA((5,))],
+        compiler_params=pltpu.CompilerParams(collective_id=cid, has_side_effects=True, vmem_limit_bytes=32 << 20),
+        cost_estimate=pl.CostEstimate(flops=0, bytes_accessed=100 << 20, transcendentals=0),
+        name="start_gather",
+    )(w_qkv, w_up, w_out, tokens, vectors)
 
 
 def pack_heads(block, b, c):
@@ -747,49 +921,30 @@
     width = tokens.shape[2]
     valid = lengths[assign[x]].astype(jnp.int32)
 
-    qkv = w_qkv.reshape(32, 3, 2, 2, 2, 2, HD)
-    qk_ranks = qkv[:, :2].transpose(3, 5, 0, 2, 4, 1, 6).reshape(2, 2, 32, 512)
-    v_ranks = qkv[:, 2].transpose(2, 4, 0, 1, 3, 5).reshape(2, 2, 32, 256)
-    qkv_block = to_ranks(jnp.concatenate([qk_ranks, v_ranks], 3), b, c)
-    small = jnp.concatenate([qv_bias.reshape(-1), out_bias, down_bias, norm_gain.reshape(-1), norm_shift.reshape(-1), up_bias])
-    small = jnp.pad(small.reshape(4, 128), ((0, 12), (0, 0)))
-    small_core, small_near = flip_core(small), flip_b(small)
-    small = jnp.stack([small, small_core, small_near, flip_core(small_near)]).reshape(2, 2, 16, 128)
-
-    qkv_block = sort_ranks(qkv_block, b, c)
-    qk_one, v_one = cube_start(qkv_block[..., :512]), cube_start(qkv_block[..., 512:])
-    out_one, small = cube_start(w_out), cube_start(small)
-    rows = gather_rows(tokens[0])
-    qk_two, v_two, out_two, small = cube_one(flip_y, qk_one), cube_one(flip_x, v_one), cube_one(flip_x, out_one), cube_one(flip_y, small)
-    qk_all, v_all, out_all, small = cube_one(flip_x, qk_two), cube_one(flip_y, v_two), cube_one(flip_y, out_two), cube_one(flip_x, small)
-    wqk, wv, wo = arrange(spot, [(qk_all, True), (v_all, False), (out_all, False)])
-    wqkv, wo = jnp.concatenate([wqk.reshape(width, 512), wv.reshape(width, 256)], 1), wo.reshape(256, width)
-
-    up = w_up.reshape(32, 2, 2, 2, 2, 2, 128).transpose(2, 4, 0, 1, 3, 5, 6).reshape(2, 2, 32, 1024)
-    up_block = sort_ranks(to_ranks(after(up, qkv_block), b, c), b, c)
-    up_one, down_one = cube_start(after(up_block, qk_one)), cube_start(after(w_down, qk_one))
-    small = small.reshape(2, 2, 2, 2, 2, 16, 128).astype(f32)
-    for axis, flag in enumerate((x, y, a, b, c)):
-        small = swap_if(flag, small, axis)
-    small = small.transpose(2, 3, 1, 4, 0, 5, 6)[..., :4, :]
-    vectors = small[..., :3, :].reshape(32, 12, 32).transpose(1, 0, 2).reshape(12, width)
+    small = jnp.concatenate([qv_bias, out_bias[None], down_bias[None], norm_gain, norm_shift], 0)
+    small = jnp.concatenate([jnp.pad(small, ((0, 0), (0, 96))), up_bias[None], jnp.zeros((3, 128), bf16)], 0)
+    wqkv, wo, up_one, rows, small = start_gather(w_qkv, w_up, w_out, tokens[0], small, 6)
+    wqkv, wo, rows = wqkv.reshape(width, 768), wo.reshape(256, width), rows.reshape(512, width)
+    down_one = cube_start(after(w_down, wqkv))
+
+    vectors = small[..., :12, :32].reshape(32, 12, 32).transpose(1, 0, 2).reshape(12, width).astype(f32)
     qv_half = pick(pick(vectors[:2].reshape(2, 2, 2, 2, 2, HD), b, 2), c, 3).reshape(2, 4, HD)
     qk_shift = jnp.concatenate([qv_half[0], jnp.zeros((4, HD), f32)], 1).reshape(512)
     v_shift = qv_half[1].reshape(256)
     out_full, down_full, gains, shifts = vectors[2], vectors[3], vectors[4:8], vectors[8:12]
-    up_shift = pick(pick(small[..., 3, :], b, 1), c, 2).reshape(1024)
+    up_shift = pick(pick(small[..., 12, :], b, 1), c, 2).reshape(1024).astype(f32)
 
     hidden = tokens[0].astype(f32)
     first = norm_rows(rows.astype(f32), gains[0], shifts[0]).astype(bf16)
-    up_two, down_two = cube_one(flip_x, up_one), cube_one(flip_y, down_one)
-    first = after(first, up_one, down_one)
+    up_two = cube_one(flip_x, up_one)
     projected = (dot_nn(first, wqkv) + jnp.concatenate([qk_shift, v_shift])).astype(bf16)
     qk, v = projected[:, :512], projected[:, 512:]
     qk = sort_ranks(qk.reshape(2, 2, 128, 4, 128), b, c).transpose(3, 0, 1, 2, 4).reshape(4, 2, 256, 128)
-    packed = exchange(after(jnp.concatenate([qk, pack_heads(v, b, c)], 2), up_two, down_two), True, 1).reshape(8, 384, 128)
+    packed = exchange(after(jnp.concatenate([qk, pack_heads(v, b, c)], 2), up_two, down_one), True, 1).reshape(8, 384, 128)
+    down_two = cube_one(flip_y, after(down_one, packed))
+    attended = attend(valid[None], packed).reshape(2, 2, 2, 128, 128)
+    attended = exchange(after(attended, down_two), False, 2)
     down_all = cube_one(flip_x, down_two)
-    attended = attend(valid[None], packed).reshape(2, 2, 2, 128, 128)
-    attended = exchange(after(attended, down_all), False, 2)
     attended = sort_ranks(unpack_heads(attended), b, c).reshape(512, 256)
 
     up_all = cube_one(flip_y, after(up_two, attended))
@@ -863,13 +1018,10 @@
     sums_up = in_ranks(sums_up, ((1, b), (3, c)))
     terms = jnp.concatenate([vecs, sums_up, jnp.zeros((2, 2, 2, 2, 2, 4, 128), f32)], 5)
     r_qkv, r_out, r_up, r_down, small = reduce_all(gw_qkv, gw_out, up_sum[:, :, 0, :, 0], down_sum[:, 0, 0], terms, 5)
-    r_up = r_up.reshape(2, 2, 32, 2, 2, 2, 128).transpose(2, 3, 0, 4, 1, 5, 6).reshape(32, 4096)
-    out_qk = r_qkv[..., :512].reshape(2, 2, 32, 2, 2, 2, HD).transpose(2, 5, 3, 0, 4, 1, 6).reshape(32, 2048)
-    out_v = r_qkv[..., 512:].reshape(2, 2, 32, 2, 2, HD).transpose(2, 3, 0, 4, 1, 5).reshape(32, 1024)
     vectors = small[:3].reshape(12, 32)
 
     return (
-        output[None], input_grad[None], jnp.concatenate([out_qk, out_v], 1), vectors[:2], r_out,
+        output[None], input_grad[None], r_qkv, vectors[:2], r_out,
         vectors[2], r_up, small[3], r_down, vectors[3], vectors[4:8], vectors[8:12])
 
 

time: 408 us -> 398 us (0.975)
  Pallas kernels: 128 us -> 174 us
  waiting for transfers between devices: 94.8 us -> 57 us
  starting transfers between devices: 47.6 us -> 17.7 us
  local copies, waits for them, and re-layouts: 56.6 us -> 73 us
    pallas_call x1 -> x2, Pallas kernels: 41 us -> 78 us  [the longest x1 41.3 us: reduce_all(): pl.pallas_call(reduce_kernel, out_shape=(S((q[0], 4 * q[1]), f32), S((o[0...]
    ppermute x47 -> x26, waiting for transfers between devices: 90.7 us -> 57 us  [flip(): return lax.ppermute(block, 'seq', [(s, s ^ bits) for s in range(16)])]
    ppermute x47 -> x26, starting transfers between devices: 38.4 us -> 13.7 us  [flip(): return lax.ppermute(block, 'seq', [(s, s ^ bits) for s in range(16)])]
    unnamed x161 -> x182, local copies, waits for them, and re-layouts: 13.4 us -> 24.4 us
    pallas_call x4, Pallas kernels: 64.1 us -> 74.6 us  [exchange(): pl.pallas_call(functools.partial(exchange_kernel, scatter), out_shape=jax...]
    concatenate x11, local copies, waits for them, and re-layouts: 3.82 us -> 9.88 us  [fast_body(): vecs = jnp.concatenate([head_sums(grad_qk), head_sums(grad_v), whole], 0)]
    reshape x15 -> x2, local copies, waits for them, and re-layouts: 7.32 us -> 1.94 us  [unpack_heads(): packed.reshape(4, 2, 128, 2, HD).transpose(1, 3, 2, 0, 4)]
    ppermute x8 -> x4, starting transfers between devices: 9.18 us -> 3.91 us  [flip_x(): return lax.ppermute(block, 'dp', [(0, 1), (1, 0)])]
  transfers between devices with their start and end apart: 55 -> 30, of which waited for: 26 -> 12; matrix products, arithmetic and copies ran while one was open for 16% -> 18% of each run, Pallas kernels for 19% -> 14%
where the time goes in v3:
time: 398 us; the launch traced here: 393 us
  Pallas kernels  174 us (44%)
  local copies, waits for them, and re-layouts  73 us (18%)
  waiting for transfers between devices  57 us (14%)
  other arithmetic  40.2 us (10%)
  matrix products  26.9 us (7%)
  starting transfers between devices  17.7 us (4%)
  between operations  4.07 us (1%)
    pallas_call x4, Pallas kernels, exchange(): pl.pallas_call(functools.partial(exchange_kernel, scatter), out_shape=jax...  74.6 us
    ppermute x26, waiting for transfers between devices, flip(): return lax.ppermute(block, 'seq', [(s, s ^ bits) for s in range(16)])  57 us
    pallas_call x1, Pallas kernels, reduce_all(): pl.pallas_call(reduce_kernel, out_shape=(S((q[0], 4 * q[1]), f32), S((o[0...  41.3 us
    pallas_call x1, Pallas kernels, start_gather(): pl.pallas_call(start_kernel, out_shape=(S(2, 2, 2, 2, 2, 32, 768), S(2, 2...  36.7 us
    unnamed x182, local copies, waits for them, and re-layouts  24.4 us
    ppermute x26, starting transfers between devices, flip(): return lax.ppermute(block, 'seq', [(s, s ^ bits) for s in range(16)])  13.7 us
    pallas_call x1, Pallas kernels, attend_back(): pl.pallas_call(attend_back_kernel, out_shape=jax.ShapeDtypeStruct(packed....  11.6 us
    dot_general x4, matrix products, dot_nn(): return jnp.dot(a, b, preferred_element_type=jnp.float32)  11.5 us
  transfers between devices with their start and end apart: 30, of which 12 were waited for; matrix products, arithmetic and copies ran while one was open for 18% of the time, Pallas kernels for 14%

profile of v3, /device:TPU:0, one launch (start us, length us, event | category | flops | bytes accessed | tf_op | source)
XLA Modules:
  0.0 392.6 jit_solution(2472828648519458615)
XLA Ops:
  6.6 36.7 %start_gather.1 = (bf16[2,2,2,2,2,32,768]{6,5,4,3,2,1,0:T(8,128)(2,1)S(1)}, bf16[2,2,2,32,1024]{4,3,2,1,0:T(8,128)(2,1)S(1)}, bf16[2,2,2,32,1024]{4,3,2,1,0:T(8,...) custom-call(bf16[32,3072]{1,0:T(8,128)(2,1)S(1)} %copy-done.13, ...), custom_call_target="tpu_custom_call" | custom-call | bytes 104857600 | tf_op jit(solution)/shard_map/start_gather/pallas_call | solution.py:893
  52.1 2.2 rev.39
  58.2 1.9 constant_dynamic-update-slice_fusion
  60.1 23.4 %exchange.4 = bf16[2,2,2,384,128]{4,3,2,1,0:T(8,128)(2,1)} custom-call(bf16[4,2,384,128]{3,2,1,0:T(8,128)(2,1)} %pad_maximum_fusion.5.src), custom_call_target="tpu_custom_call" | custom-call | bytes 38400000 | tf_op jit(solution)/shard_map/exchange/pallas_call | solution.py:336
  88.4 8.0 %attend.1 = bf16[8,128,128]{2,1,0:T(8,128)(2,1)S(1)} custom-call(s32[1]{0:T(128)} %dynamic_slice.47.valid_ref, bf16[8,384,128]{2,1,0:T(8,128)(2,1)S(1)} %bitcast.225), custom_call_target="tpu_custom_call" | custom-call | tf_op jit(solution)/shard_map/attend/pallas_call | solution.py:432
  98.3 18.5 %exchange.5 = bf16[4,2,128,128]{3,2,1,0:T(8,128)(2,1)} custom-call(bf16[2,2,2,128,128]{4,3,2,1,0:T(8,128)(2,1)} %bitcast.232), custom_call_target="tpu_custom_call" | custom-call | bytes 12800000 | tf_op jit(solution)/shard_map/exchange/pallas_call | solution.py:336
  122.4 2.9 collective-permute-start.5
  137.1 1.8 collective-permute-start.7
  140.3 4.7 %collective-permute-done.7 = bf16[128,1024]{1,0:T(8,128)(2,1)} collective-permute-done((bf16[128,1024]{1,0:T(8,128)(2,1)}, bf16[128,1024]{1,0:T(8,128)(2,1)}, u32[]{:S(2)}, u32[]{:S(2)}) %collective-permute-start.7) | collective-permute-done | bytes 262176 | tf_op jit(solution)/shard_map/ppermute | solution.py:457
  145.0 12.2 %collective-permute-done.9 = bf16[4,2,2,32,1024]{4,3,2,1,0:T(8,128)(2,1)} collective-permute-done((bf16[4,2,2,32,1024]{4,3,2,1,0:T(8,128)(2,1)}, bf16[4,2,2,32,1024]{4,3,2,1,0:T(8,128)(2,1)}, u32[]{:S(2)}, u32[]{:S(2)}) %collective-permute-start.9) | collective-permute-done | bytes 1048608 | tf_op jit(solution)/shard_map/ppermute | solution.py:457
  162.1 8.8 %multiply_convert_fusion = (bf16[512,1024]{1,0:T(8,128)(2,1)S(1)}, f32[512,1024]{1,0:T(8,128)}, f32[512,1024]{1,0:T(8,128)}) fusion(f32[1024]{0:T(1024)S(1)} %bitcast.264, bf16[1024,1024]{1,0:T(8,128)(2,1)S(1)} %bitcast.237, bf16[128,1024]{1,0:T(8,128)(2,1)S(1)} %collective-permute-done.8, bf16[128,1024]{1,0:T(8,128)(2,1)} %collective-permute-done.7, ...), kind=kOutput, calls=%fused_computation.13 | convolution fusion | flops 1112539136 | bytes 8392704 | tf_op jit(solution)/shard_map/dot_general | solution.py:351
  176.9 6.8 %collective-permute-done.13 = bf16[128,1024]{1,0:T(8,128)(2,1)} collective-permute-done((bf16[128,1024]{1,0:T(8,128)(2,1)S(1)}, bf16[128,1024]{1,0:T(8,128)(2,1)}, u32[]{:S(2)}, u32[]{:S(2)}) %collective-permute-start.13) | collective-permute-done | bytes 262176 | tf_op jit(solution)/shard_map/ppermute | solution.py:457
  187.7 6.7 %collective-permute-done.15 = bf16[128,1024]{1,0:T(8,128)(2,1)S(1)} collective-permute-done((bf16[128,1024]{1,0:T(8,128)(2,1)S(1)}, bf16[128,1024]{1,0:T(8,128)(2,1)S(1)}, u32[]{:S(2)}, u32[]{:S(2)}) %collective-permute-start.15) | collective-permute-done | bytes 262176 | tf_op jit(solution)/shard_map/ppermute | solution.py:457
  195.9 2.6 convolution_convert_fusion.1
  200.1 2.0 convert_reduce_fusion
  202.1 3.8 convolution_convert_fusion
  218.3 3.6 collective-permute-done.19
  229.5 2.5 collective-permute-done.21
  232.0 9.8 %collective-permute-done.23 = bf16[2,1,2,128,1024]{4,3,0,2,1:T(8,128)(2,1)} collective-permute-done((bf16[2,1,2,128,1024]{4,3,0,2,1:T(8,128)(2,1)}, bf16[2,1,2,128,1024]{4,3,0,2,1:T(8,128)(2,1)}, u32[]{:S(2)}, u32[]{:S(2)}) %collective-permute-start.23) | collective-permute-done | bytes 1048608 | tf_op jit(solution)/shard_map/ppermute | solution.py:457
  241.8 2.6 add_convert_fusion.1
  249.3 10.8 %exchange.6 = bf16[2,2,2,128,128]{4,3,2,1,0:T(8,128)(2,1)} custom-call(bf16[4,2,128,128]{3,2,1,0:T(8,128)(2,1)} %copy.49.src), custom_call_target="tpu_custom_call" | custom-call | bytes 12800000 | tf_op jit(solution)/shard_map/exchange/pallas_call | solution.py:336
  267.8 1.9 constant_dynamic-slice_fusion.1
  270.3 11.6 %attend_back.1 = bf16[8,384,128]{2,1,0:T(8,128)(2,1)S(1)} custom-call(s32[1]{0:T(128)} %dynamic_slice.47.valid_ref, bf16[8,384,128]{2,1,0:T(8,128)(2,1)S(1)} %bitcast.226, bf16[8,128,128]{2,1,0:T(8,128)(2,1)S(1)} %bitcast.231), custom_call_target="tpu_custom_call" | custom-call | tf_op jit(solution)/shard_map/attend_back/pallas_call | solution.py:445
  281.9 1.8 convolution_convert_fusion.3
  283.9 21.9 %exchange.7 = bf16[4,2,384,128]{3,2,1,0:T(8,128)(2,1)} custom-call(bf16[2,2,2,384,128]{4,3,2,1,0:T(8,128)(2,1)} %bitcast.228), custom_call_target="tpu_custom_call" | custom-call | bytes 38400000 | tf_op jit(solution)/shard_map/exchange/pallas_call | solution.py:336
  310.6 1.8 copy.56
  320.8 2.5 convolution_convert_fusion.2
  323.3 6.2 %collective-permute-done.28 = bf16[128,1024]{1,0:T(8,128)(2,1)S(1)} collective-permute-done((bf16[128,1024]{1,0:T(8,128)(2,1)S(1)}, bf16[128,1024]{1,0:T(8,128)(2,1)S(1)}, u32[]{:S(2)}, u32[]{:S(2)}) %collective-permute-start.28) | collective-permute-done | bytes 262176 | tf_op jit(solution)/shard_map/ppermute | solution.py:457
  333.9 3.0 concatenate.94
  338.8 41.3 %reduce_all.1 = (f32[32,3072]{1,0:T(8,128)S(1)}, f32[32,1024]{1,0:T(8,128)S(1)}, f32[32,4096]{1,0:T(8,128)S(1)}, f32[128,1024]{1,0:T(8,128)S(1)}, f32[8,128]{1,0:T(8,128)S(1)}) custom-call(bf16[2,2,2,2,2,32,768]{6,5,4,3,2,1,0:T(8,128)(2,1)S(1)} %bitcast.230, bf16[2,2,2,32,1024]{4,3,2,1,0:T(8,128)(2,1)S(1)} %bitcast.233, ...), custom_call_target="tpu_custom_call" | custom-call | tf_op jit(solution)/shard_map/reduce_all/pallas_call | solution.py:736
  384.9 2.2 fusion.55
  388.4 1.8 copy.78
  (387 shorter events, 120.4 us)
Async XLA Ops:
  44.5 12.7 %collective-permute-start.1 = (bf16[128,1024]{1,0:T(8,128)(2,1)}, bf16[128,1024]{1,0:T(8,128)(2,1)}, u32[]{:S(2)}, u32[]{:S(2)}) collective-permute-start(bf16[128,1024]{1,0:T(8,128)(2,1)} %param.24), channel_id=1, source_target_pairs={{0,16},{2,18},{4,20},{6,22},{8,24},{10,26},{12,28},{14,30},{16,0},... | collective-permute-start | bytes 786440 | tf_op jit(solution)/shard_map/ppermute | solution.py:457
  44.5 13.7 %collective-permute-start = (bf16[2,2,2,32,1024]{4,3,2,1,0:T(8,128)(2,1)S(1)}, bf16[2,2,2,32,1024]{4,3,2,1,0:T(8,128)(2,1)}, u32[]{:S(2)}, u32[]{:S(2)}) collective-permute-start(bf16[2,2,2,32,1024]{4,3,2,1,0:T(8,128)(2,1)S(1)} %get-tuple-element.37), channel_id=1, source_target_pairs={{0,1},{1,0},{2,3},{3,2},{4,5},{5,4},{6,7},{7,6},{8,9},{9,8},{10,11... | collective-permute-start | bytes 1572872 | tf_op jit(solution)/shard_map/ppermute | solution.py:464
  83.5 13.7 %collective-permute-start.2 = (bf16[2,128,1024]{2,1,0:T(8,128)(2,1)S(1)}, bf16[2,128,1024]{2,1,0:T(8,128)(2,1)}, u32[]{:S(2)}, u32[]{:S(2)}) collective-permute-start(bf16[2,128,1024]{2,1,0:T(8,128)(2,1)S(1)} %pad_maximum_fusion.6), channel_id=1, source_target_pairs={{0,4},{2,6},{4,0},{6,2},{8,12},{10,14},{12,8},{14,10},{16,20},{18,... | collective-permute-start | bytes 1572872 | tf_op jit(solution)/shard_map/ppermute | solution.py:457
  119.7 1.9 collective-permute-start.4
  119.7 13.3 %collective-permute-start.3 = (f32[128,1024]{1,0:T(8,128)}, f32[128,1024]{1,0:T(8,128)S(1)}, u32[]{:S(2)}, u32[]{:S(2)}) collective-permute-start(f32[128,1024]{1,0:T(8,128)} %get-tuple-element.109), channel_id=1, source_target_pairs={{0,2},{2,0},{4,6},{6,4},{8,10},{10,8},{12,14},{14,12},{16,18},{18,... | collective-permute-start | bytes 1572872 | tf_op jit(solution)/shard_map/ppermute | solution.py:457
  122.4 10.6 %collective-permute-start.5 = (bf16[128,1024]{1,0:T(8,128)(2,1)}, bf16[128,1024]{1,0:T(8,128)(2,1)}, u32[]{:S(2)}, u32[]{:S(2)}) collective-permute-start(bf16[128,1024]{1,0:T(8,128)(2,1)} %fusion.40), channel_id=1, source_target_pairs={{0,8},{2,10},{4,12},{6,14},{8,0},{10,2},{12,4},{14,6},{16,24},{18,... | collective-permute-start | bytes 786440 | tf_op jit(solution)/shard_map/ppermute | solution.py:457
  131.1 27.9 %collective-permute-start.10 = (bf16[4,128,1024]{2,1,0:T(8,128)(2,1)}, bf16[4,128,1024]{2,1,0:T(8,128)(2,1)}, u32[]{:S(2)}, u32[]{:S(2)}) collective-permute-start(bf16[4,128,1024]{2,1,0:T(8,128)(2,1)} %copy-done.40), channel_id=1, source_target_pairs={{0,1},{1,0},{2,3},{3,2},{4,5},{5,4},{6,7},{7,6},{8,9},{9,8},{10,11... | collective-permute-start | bytes 3145736 | tf_op jit(solution)/shard_map/ppermute | solution.py:464
  132.3 25.0 %collective-permute-start.9 = (bf16[4,2,2,32,1024]{4,3,2,1,0:T(8,128)(2,1)}, bf16[4,2,2,32,1024]{4,3,2,1,0:T(8,128)(2,1)}, u32[]{:S(2)}, u32[]{:S(2)}) collective-permute-start(bf16[4,2,2,32,1024]{4,3,2,1,0:T(8,128)(2,1)} %constant_dynamic-update-slice_fusion), channel_id=1, source_target_pairs={{0,4},{2,6},{4,0},{6,2},{8,12},{10,14},{12,8},{14,10},{16,20},{18,... | collective-permute-start | bytes 3145736 | tf_op jit(solution)/shard_map/ppermute | solution.py:457
  137.1 7.9 %collective-permute-start.7 = (bf16[128,1024]{1,0:T(8,128)(2,1)}, bf16[128,1024]{1,0:T(8,128)(2,1)}, u32[]{:S(2)}, u32[]{:S(2)}) collective-permute-start(bf16[128,1024]{1,0:T(8,128)(2,1)} %add_convert_fusion.11), channel_id=1, source_target_pairs={{0,8},{2,10},{4,12},{6,14},{8,0},{10,2},{12,4},{14,6},{16,24},{18,... | collective-permute-start | bytes 786440 | tf_op jit(solution)/shard_map/ppermute | solution.py:457
  140.3 21.8 %collective-permute-start.6 = (bf16[128,1024]{1,0:T(8,128)(2,1)}, bf16[128,1024]{1,0:T(8,128)(2,1)S(1)}, u32[]{:S(2)}, u32[]{:S(2)}) collective-permute-start(bf16[128,1024]{1,0:T(8,128)(2,1)} %add_convert_fusion.11), channel_id=1, source_target_pairs={{0,2},{2,0},{4,6},{6,4},{8,10},{10,8},{12,14},{14,12},{16,18},{18,... | collective-permute-start | bytes 786440 | tf_op jit(solution)/shard_map/ppermute | solution.py:457
  145.0 17.1 %collective-permute-start.8 = (bf16[128,1024]{1,0:T(8,128)(2,1)}, bf16[128,1024]{1,0:T(8,128)(2,1)S(1)}, u32[]{:S(2)}, u32[]{:S(2)}) collective-permute-start(bf16[128,1024]{1,0:T(8,128)(2,1)} %collective-permute-done.7), channel_id=1, source_target_pairs={{0,2},{2,0},{4,6},{6,4},{8,10},{10,8},{12,14},{14,12},{16,18},{18,... | collective-permute-start | bytes 786440 | tf_op jit(solution)/shard_map/ppermute | solution.py:457
  173.2 1.9 collective-permute-start.12
  173.2 3.7 collective-permute-start.11
  175.1 8.5 %collective-permute-start.13 = (bf16[128,1024]{1,0:T(8,128)(2,1)S(1)}, bf16[128,1024]{1,0:T(8,128)(2,1)}, u32[]{:S(2)}, u32[]{:S(2)}) collective-permute-start(bf16[128,1024]{1,0:T(8,128)(2,1)S(1)} %fusion.35), channel_id=1, source_target_pairs={{0,8},{2,10},{4,12},{6,14},{8,0},{10,2},{12,4},{14,6},{16,24},{18,... | collective-permute-start | bytes 786440 | tf_op jit(solution)/shard_map/ppermute | solution.py:457
  186.8 7.6 %collective-permute-start.15 = (bf16[128,1024]{1,0:T(8,128)(2,1)S(1)}, bf16[128,1024]{1,0:T(8,128)(2,1)S(1)}, u32[]{:S(2)}, u32[]{:S(2)}) collective-permute-start(bf16[128,1024]{1,0:T(8,128)(2,1)S(1)} %get-tuple-element.73), channel_id=1, source_target_pairs={{0,8},{2,10},{4,12},{6,14},{8,0},{10,2},{12,4},{14,6},{16,24},{18,... | collective-permute-start | bytes 786440 | tf_op jit(solution)/shard_map/ppermute | solution.py:457
  187.7 6.7 %collective-permute-start.14 = (bf16[128,1024]{1,0:T(8,128)(2,1)S(1)}, bf16[128,1024]{1,0:T(8,128)(2,1)S(1)}, u32[]{:S(2)}, u32[]{:S(2)}) collective-permute-start(bf16[128,1024]{1,0:T(8,128)(2,1)S(1)} %get-tuple-element.73), channel_id=1, source_target_pairs={{0,2},{2,0},{4,6},{6,4},{8,10},{10,8},{12,14},{14,12},{16,18},{18,... | collective-permute-start | bytes 786440 | tf_op jit(solution)/shard_map/ppermute | solution.py:457
  194.4 1.5 collective-permute-start.16
  209.6 2.6 collective-permute-start.18
  211.8 6.5 %collective-permute-start.17 = (f32[128,1024]{1,0:T(8,128)}, f32[128,1024]{1,0:T(8,128)S(1)}, u32[]{:S(2)}, u32[]{:S(2)}) collective-permute-start(f32[128,1024]{1,0:T(8,128)} %get-tuple-element.105), channel_id=1, source_target_pairs={{0,2},{2,0},{4,6},{6,4},{8,10},{10,8},{12,14},{14,12},{16,18},{18,... | collective-permute-start | bytes 1572872 | tf_op jit(solution)/shard_map/ppermute | solution.py:457
  213.4 8.4 %collective-permute-start.19 = (bf16[128,1024]{1,0:T(8,128)(2,1)S(1)}, bf16[128,1024]{1,0:T(8,128)(2,1)S(1)}, u32[]{:S(2)}, u32[]{:S(2)}) collective-permute-start(bf16[128,1024]{1,0:T(8,128)(2,1)S(1)} %fusion.31), channel_id=1, source_target_pairs={{0,8},{2,10},{4,12},{6,14},{8,0},{10,2},{12,4},{14,6},{16,24},{18,... | collective-permute-start | bytes 786440 | tf_op jit(solution)/shard_map/ppermute | solution.py:457
  216.6 25.2 %collective-permute-start.23 = (bf16[2,1,2,128,1024]{4,3,0,2,1:T(8,128)(2,1)}, bf16[2,1,2,128,1024]{4,3,0,2,1:T(8,128)(2,1)}, u32[]{:S(2)}, u32[]{:S(2)}) collective-permute-start(bf16[2,1,2,128,1024]{4,3,0,2,1:T(8,128)(2,1)} %copy.62), channel_id=1, source_target_pairs={{0,4},{2,6},{4,0},{6,2},{8,12},{10,14},{12,8},{14,10},{16,20},{18,... | collective-permute-start | bytes 3145736 | tf_op jit(solution)/shard_map/ppermute | solution.py:457
  224.4 7.7 %collective-permute-start.21 = (bf16[128,1024]{1,0:T(8,128)(2,1)S(1)}, bf16[128,1024]{1,0:T(8,128)(2,1)S(1)}, u32[]{:S(2)}, u32[]{:S(2)}) collective-permute-start(bf16[128,1024]{1,0:T(8,128)(2,1)S(1)} %get-tuple-element.75), channel_id=1, source_target_pairs={{0,8},{2,10},{4,12},{6,14},{8,0},{10,2},{12,4},{14,6},{16,24},{18,... | collective-permute-start | bytes 786440 | tf_op jit(solution)/shard_map/ppermute | solution.py:457
  226.6 33.5 %collective-permute-start.24 = (bf16[2,2,2,2,1,32,1024]{6,5,3,1,0,4,2:T(8,128)(2,1)}, bf16[2,2,2,2,1,32,1024]{6,5,3,1,0,4,2:T(8,128)(2,1)}, u32[]{:S(2)}, u32[]{:S(2)}) collective-permute-start(bf16[2,2,2,2,1,32,1024]{6,5,3,1,0,4,2:T(8,128)(2,1)} %copy.64), channel_id=1, source_target_pairs={{0,1},{1,0},{2,3},{3,2},{4,5},{5,4},{6,7},{7,6},{8,9},{9,8},{10,11... | collective-permute-start | bytes 3145736 | tf_op jit(solution)/shard_map/ppermute | solution.py:464
  229.5 14.9 %collective-permute-start.20 = (bf16[128,1024]{1,0:T(8,128)(2,1)S(1)}, bf16[128,1024]{1,0:T(8,128)(2,1)S(1)}, u32[]{:S(2)}, u32[]{:S(2)}) collective-permute-start(bf16[128,1024]{1,0:T(8,128)(2,1)S(1)} %get-tuple-element.75), channel_id=1, source_target_pairs={{0,2},{2,0},{4,6},{6,4},{8,10},{10,8},{12,14},{14,12},{16,18},{18,... | collective-permute-start | bytes 786440 | tf_op jit(solution)/shard_map/ppermute | solution.py:457
  232.0 12.4 %collective-permute-start.22 = (bf16[128,1024]{1,0:T(8,128)(2,1)S(1)}, bf16[128,1024]{1,0:T(8,128)(2,1)S(1)}, u32[]{:S(2)}, u32[]{:S(2)}) collective-permute-start(bf16[128,1024]{1,0:T(8,128)(2,1)S(1)} %collective-permute-done.21), channel_id=1, source_target_pairs={{0,2},{2,0},{4,6},{6,4},{8,10},{10,8},{12,14},{14,12},{16,18},{18,... | collective-permute-start | bytes 786440 | tf_op jit(solution)/shard_map/ppermute | solution.py:457
  262.9 20.8 %collective-permute-start.25 = (bf16[2,2,1,2,1,32,1024]{6,5,3,1,0,4,2:T(8,128)(2,1)S(1)}, bf16[2,2,1,2,1,32,1024]{6,5,3,1,0,4,2:T(8,128)(2,1)S(1)}, u32[]{:S(2)}, u32[]{:S(2)}) collective-permute-start(bf16[2,2,1,2,1,32,1024]{6,5,3,1,0,4,2:T(8,128)(2,1)S(1)} %constant_dynamic-slice_fusion.2), channel_id=1, source_target_pairs={{0,4},{2,6},{4,0},{6,2},{8,12},{10,14},{12,8},{14,10},{16,20},{18,... | collective-permute-start | bytes 1572872 | tf_op jit(solution)/shard_map/ppermute | solution.py:457
  269.7 46.0 %collective-permute-start.29 = (bf16[2,1,1,128,1024]{4,3,0,2,1:T(8,128)(2,1)}, bf16[2,1,1,128,1024]{4,3,0,2,1:T(8,128)(2,1)}, u32[]{:S(2)}, u32[]{:S(2)}) collective-permute-start(bf16[2,1,1,128,1024]{4,3,0,2,1:T(8,128)(2,1)} %constant_dynamic-slice_fusion.1), channel_id=1, source_target_pairs={{0,1},{1,0},{2,3},{3,2},{4,5},{5,4},{6,7},{7,6},{8,9},{9,8},{10,11... | collective-permute-start | bytes 1572872 | tf_op jit(solution)/shard_map/ppermute | solution.py:464
  315.7 3.9 collective-permute-start.27
  319.6 3.7 collective-permute-start.26
  320.7 8.8 %collective-permute-start.28 = (bf16[128,1024]{1,0:T(8,128)(2,1)S(1)}, bf16[128,1024]{1,0:T(8,128)(2,1)S(1)}, u32[]{:S(2)}, u32[]{:S(2)}) collective-permute-start(bf16[128,1024]{1,0:T(8,128)(2,1)S(1)} %fusion.27), channel_id=1, source_target_pairs={{0,8},{2,10},{4,12},{6,14},{8,0},{10,2},{12,4},{14,6},{16,24},{18,... | collective-permute-start | bytes 786440 | tf_op jit(solution)/shard_map/ppermute | solution.py:457
  333.9 51.0 %copy-start.65 = (f32[128]{0:T(128)S(1)}, f32[128]{0:T(128)}, u32[]{:S(2)}) copy-start(f32[128]{0:T(128)} %copy-done.64) | copy-start | bytes 1540
  333.9 51.0 %copy-start.67 = (f32[128]{0:T(128)S(1)}, f32[128]{0:T(128)}, u32[]{:S(2)}) copy-start(f32[128]{0:T(128)} %copy-done.66) | copy-start | bytes 1540
  (86 other events, 481.5 us)
